TPU v7x, 128 devices: a whole 4x4x4 slice. The times are simulated.
128 devices in a mesh: mem: 8 (over z, y_lo), lev: 16 (over y_hi, x, core).
Axes of the slice: x: 4, y: 4 (y_hi: 2, y_lo: 2; y = y_hi * 2 + y_lo), z: 4, core: 2. Of those that a mesh axis runs over, the one named last changes fastest.
Arguments:
- control: float32 [8, 64, 200, 400], P('mem', 'lev'), may hold values from -6 to 6
- perturbations: bfloat16 [8, 2, 2, 64, 80000], P('mem', None, None, None, 'lev'), may hold values from -4 to 4
- member_scales: float32 [8], P('mem'), may hold values from 0.05 to 0.2
- vertical_loc: float32 [64, 64], replicated, may hold values from -0.75 to 0.75
- latitude_loc: float32 [200, 200], replicated, may hold values from -0.4375 to 0.4375
- longitude_loc: float32 [400, 400], replicated, may hold values from -0.3125 to 0.3125
- observed_index: int32 [2, 65536], P(None, 'lev'), may hold values from 0 to 639999
- observed_weight: float32 [2, 65536], P(None, 'lev'), may hold values from 0.5 to 8
Outputs:
- hessian_vector: float32 [8, 64, 200, 400], P('mem', 'lev')
All inputs are finite; a program needn't handle non-finite values.
Results may differ from a plain program's by a relative error of at most 0.0003.
Values sent between devices are 32-bit elements; how exact they have to be, the bound alone decides.
No kernel may reach another device: no remote copies, remote signals or barrier semaphores. Data moves between devices by JAX's collectives and lax.ppermute only.
A program may use at most 192 MiB of HBM per device.

v0:
```python
import jax
import jax.numpy as jnp
from jax import lax
from jax.sharding import PartitionSpec as P

HIGH = lax.Precision.HIGHEST


def body(
    control,
    perturbations,
    member_scales,
    vertical_loc,
    latitude_loc,
    longitude_loc,
    observed_index,
    observed_weight,
):
    members, level_count, lat_size, lon_size = control.shape
    rows = jnp.einsum("ab,mlbq->mlaq", latitude_loc, control, precision=HIGH)
    horizontal = jnp.einsum("mlaq,oq->mlao", rows, longitude_loc, precision=HIGH)
    flat_fields = horizontal.reshape(members, level_count, lat_size * lon_size)
    columns = lax.all_to_all(flat_fields, "lev", split_axis=2, concat_axis=1, tiled=True)
    localized = jnp.einsum("lk,mkp->mlp", vertical_loc, columns, precision=HIGH)
    scaled = localized * member_scales[:, None, None]
    slot_count, var_count = (perturbations.shape[1], perturbations.shape[2])
    all_levels, column_width = (perturbations.shape[3], perturbations.shape[4])
    span = all_levels * column_width
    slot_rows = jnp.arange(slot_count, dtype=jnp.int32)[:, None]
    partial_value = perturbations[0].astype(jnp.float32) * scaled[0][None, None]
    obs_grid = jnp.zeros((slot_count, var_count * span), jnp.float32)
    obs_grid = obs_grid.at[slot_rows, observed_index].add(observed_weight)
    obs_grid = obs_grid.reshape(slot_count, var_count, all_levels, column_width)
    increment = lax.psum(partial_value, "mem")
    innovation_adj = obs_grid * increment
    summed = jnp.sum(perturbations[0].astype(jnp.float32) * innovation_adj, axis=(0, 1))
    adjoint_list = [summed * member_scales[0]]
    member_adj = jnp.stack(adjoint_list, axis=0)
    vertical_adj = jnp.einsum("kl,mkp->mlp", vertical_loc, member_adj, precision=HIGH)
    level_fields = lax.all_to_all(vertical_adj, "lev", split_axis=1, concat_axis=2, tiled=True)
    level_fields = level_fields.reshape(members, level_count, lat_size, lon_size)
    back_rows = jnp.einsum("ba,mlbq->mlaq", latitude_loc, level_fields, precision=HIGH)
    return control + jnp.einsum("mlaq,qo->mlao", back_rows, longitude_loc, precision=HIGH)


def solution(mesh):
    placed = (
        P("mem", "lev", None, None),
        P("mem", None, None, None, "lev"),
        P("mem"),
        P(),
        P(),
        P(),
        P(None, "lev"),
        P(None, "lev"),
    )
    return jax.shard_map(
        body, mesh=mesh, in_specs=placed, out_specs=P("mem", "lev", None, None), check_vma=False
    )
```

profile of v0, /device:TPU:1, one launch (start us, length us, event | category | flops | bytes accessed | tf_op | source)
XLA Modules:
  0.0 873.8 jit_solution(12977082701842625879)
XLA Ops:
  6.5 0.0 copy-start
  6.5 4.9 fusion.8
  11.4 0.0 copy-done
  11.4 6.5 fusion.6
  17.9 23.7 %copy.36 = f32[4,200,400]{0,2,1:T(8,128)} copy(f32[4,200,400]{2,1,0:T(8,128)S(1)} %fusion.6) | data formatting | bytes 2560000 | tf_op jit(solution)/shard_map/reshape | solution.py:22
  41.6 0.6 broadcast.25
  42.2 371.8 %reduce.4 = f32[80000,4]{1,0:T(8,128)} reduce(f32[80000,1,4]{2,1,0:T(1,128)} %bitcast.71, f32[]{:T(128)} %broadcast.25), dimensions={1}, to_apply=%bitcast.61.reduce_sub_computation | reduce | bytes 2560004
  414.0 37.7 %reshape.67 = f32[16,1,20000]{2,1,0:T(1,128)} reshape(f32[80000,4]{1,0:T(8,128)} %reduce.4) | data formatting | bytes 2560000
  451.6 8.4 all-to-all-start
  460.1 0.2 all-reduce.2.cloned.1.call-start
  460.9 18.9 %all-to-all-done = f32[16,1,20000]{2,1,0:T(1,128)S(1)} async-done(((f32[16,1,20000]{2,1,0:T(1,128)}), f32[16,1,20000]{2,1,0:T(1,128)S(1)}, u32[]{:S(2)}, u32[]{:S(2)}) %all-to-all-start) | async-done | bytes 1280032 | tf_op jit(solution)/shard_map/all_to_all | solution.py:23
  479.9 3.7 reduce.5
  483.6 85.7 %reshape.68 = f32[80000,1,4]{2,1,0:T(1,128)} reshape(f32[16,20000]{1,0:T(8,128)S(1)} %reduce.5) | data formatting | bytes 2560000
  569.3 21.9 %copy.37 = f32[1,4,16,5000]{3,2,1,0:T(8,128)S(1)} copy(f32[1,4,16,5000]{1,3,2,0:T(8,128)} %bitcast.70) | data formatting | bytes 2560000 | tf_op jit(solution)/shard_map/all_to_all | solution.py:23
  591.2 0.8 copy.27
  592.0 0.0 copy-start.4
  592.0 1.5 reshape.48
  593.6 0.0 copy-start.1
  593.6 0.0 copy-done.4
  593.6 2.8 fusion
  596.3 0.0 copy-done.1
  596.3 3.0 convert_multiply_fusion.1
  599.3 0.0 copy-start.5
  599.3 0.0 copy-start.8
  599.3 0.0 copy-start.7
  599.3 0.0 all-reduce.2.cloned.1.call-update
  599.4 0.7 copy-done.5
  600.1 0.0 copy-done.8
  600.1 0.1 multiply_reduce_fusion
  600.2 0.0 copy-done.7
  600.2 0.1 and_reduce_fusion
  600.4 0.0 copy-done.6
  600.4 0.6 copy.39
  601.1 45.9 %scatter_custom_fusion = f32[1280000]{0:T(1024)} fusion(s32[8192]{0:T(1024)S(1)} %bitcast.76, f32[8192]{0:T(1024)} %bitcast.77, f32[]{:T(128)} %constant.3.clone.1), kind=kCustom, calls=%fused_computation.7 | custom fusion | flops 8192 | bytes 5120512
  646.9 7.2 reshape.44
  654.2 164.8 %all-reduce.2.cloned.1.call-done = f32[2,2,64,5000]{3,2,1,0:T(8,128)} async-done(((f32[2,2,64,5000]{3,2,1,0:T(8,128)}), f32[2,2,64,5000]{3,2,1,0:T(8,128)}) %all-reduce.2.cloned.1.call-update) | async-done | bytes 5120016 | tf_op jit(solution)/shard_map/psum | solution.py:34
  819.0 5.5 fusion.1
  824.5 1.4 convolution_bitcast_fusion
  825.9 1.3 copy.28
  827.2 27.5 %all_to_all.30 = f32[1,64,5000]{2,0,1:T(1,128)S(1)} all-to-all(f32[1,64,5000]{2,0,1:T(1,128)S(1)} %copy.28), channel_id=1, replica_groups=mesh['mem'=8,'lev'=16] {'lev'}, dimensions={1} | all-to-all | bytes 2560000 | tf_op jit(solution)/shard_map/all_to_all | solution.py:40
  854.7 1.8 copy.41
  856.6 0.0 copy-start.3
  856.6 2.0 reshape.49
  858.5 0.0 copy-done.3
  858.6 0.0 copy-start.2
  858.6 3.3 fusion.16
  861.9 0.0 copy-done.2
  861.9 4.8 bitcast_add_fusion
  (5 shorter events, 0.1 us)
Async XLA Ops:
  6.5 4.9 copy-start
  451.6 28.2 %all-to-all-start = ((f32[16,1,20000]{2,1,0:T(1,128)}), f32[16,1,20000]{2,1,0:T(1,128)S(1)}, u32[]{:S(2)}, u32[]{:S(2)}) async-start(f32[16,1,20000]{2,1,0:T(1,128)} %reshape.67), calls=%async_computation | async-start | bytes 2572288 | tf_op jit(solution)/shard_map/all_to_all | solution.py:23
  460.1 358.9 %all-reduce.2.cloned.1.call-start = ((), (), s32[]{:S(2)}) async-start(), calls=%async_computation.2 | async-start | bytes 10485760 | tf_op jit(solution)/shard_map/psum | solution.py:34
  592.0 1.5 copy-start.4
  593.6 2.8 copy-start.1
  599.3 0.8 copy-start.5
  599.3 0.8 copy-start.8
  599.3 0.9 copy-start.7
  599.3 1.1 copy-start.6
  856.6 2.0 copy-start.3
  858.6 3.3 copy-start.2
Sparse Core Ops, SparseCore 0:
  599.5 219.4 all-reduce.1
where the time goes:
time: 881 us; the launch traced here: 874 us
  other arithmetic  430 us (49%)
  local copies, waits for them, and re-layouts  186 us (21%)
  waiting for transfers between devices  184 us (21%)
  blocking collectives  27.5 us (3%)
  matrix products  23.6 us (3%)
  between operations  14.5 us (2%)
    unnamed x5, other arithmetic  418 us
    psum x1, waiting for transfers between devices, body(): increment = lax.psum(partial_value, 'mem')  165 us
    unnamed x23, local copies, waits for them, and re-layouts  125 us
    all_to_all x1, blocking collectives, body(): lax.all_to_all(vertical_adj, 'lev', split_axis=1, concat_axis=2, tiled=True)  27.5 us
    reshape x1, local copies, waits for them, and re-layouts, body(): flat_fields = horizontal.reshape(members, level_count, lat_size * lon_size)  23.7 us
    all_to_all x2, local copies, waits for them, and re-layouts, body(): lax.all_to_all(flat_fields, 'lev', split_axis=2, concat_axis=1, tiled=True)  22.7 us
    all_to_all x1, waiting for transfers between devices, body(): lax.all_to_all(flat_fields, 'lev', split_axis=2, concat_axis=1, tiled=True)  18.9 us
  transfers between devices with their start and end apart: 2, of which 2 were waited for; matrix products, arithmetic and copies ran while one was open for 6% of the time, Pallas kernels for 0%

commit v1 on v0

v1 whole, which is shorter than its diff:
```python
import functools

import jax
import jax.numpy as jnp
from jax import lax
from jax.experimental import pallas as pl
from jax.experimental.pallas import tpu as pltpu
from jax.sharding import PartitionSpec as P

F32 = jnp.float32
BF16 = jnp.bfloat16
I32 = jnp.int32

NB = 32
OB = 256
NK = 20
YS = 136
NN = (((1,), (0,)), ((), ()))
NT = (((1,), (1,)), ((), ()))
TN = (((0,), (0,)), ((), ()))


def split(x):
    hi = x.astype(BF16)
    return hi, (x - hi.astype(F32)).astype(BF16)


def mm(a, b, dims):
    return lax.dot_general(a, b, dims, preferred_element_type=F32)


def mm3(a, b, dims=NN):
    return mm(a[0], b[0], dims) + (mm(a[0], b[1], dims) + mm(a[1], b[0], dims))


def pad_latitude(a_ref, ap_ref):
    ap_ref[...] = jnp.zeros_like(ap_ref)
    for i in range(8):
        row = (i % 2) * 128 + (i // 2) * 32
        ap_ref[row : row + 25, :] = a_ref[25 * i : 25 * i + 25, :]


def iota(shape, dim):
    return lax.broadcasted_iota(I32, shape, dim)


def forward_kernel(c_ref, a_ref, o_ref, f_ref, ap_ref, y_ref):
    pad_latitude(a_ref, ap_ref)
    lat = split(ap_ref[...])
    lon = split(o_ref[...])
    for l in range(4):
        rows = mm3(split(c_ref[l]), lon, NT)
        field = mm3(lat, split(rows))
        for u in range(2):
            base = (4 * u + l) * YS
            part = field[128 * u : 128 * u + 128]
            for j in range(3):
                y_ref[j, base : base + 128, :] = part[:, 128 * j : 128 * j + 128]
            y_ref[3, base : base + 128, 0:16] = part[:, 384:400]

    lane = iota((8, 128), 1)
    upper = iota((8, 128), 0) < 4

    def one_w(w, carry):
        loaded = {}

        def load(r, j):
            if (r, j) not in loaded:
                loaded[(r, j)] = y_ref[j, pl.ds(w * 32 + r, 8, stride=YS), :]
            return loaded[(r, j)]

        def chunk(e, i):
            first = 5000 * e + 128 * i
            count = min(128, 5000 - 128 * i)
            done = 0
            value = None
            while done < count:
                r, o = divmod(first + done, 400)
                j, s = divmod(o, 128)
                n = min(128 - s, 400 - o, count - done)
                shift = (done - s) % 128
                piece = load(r, j)
                if shift:
                    piece = pltpu.roll(piece, shift, 1)
                value = piece if value is None else jnp.where(lane < done, value, piece)
                done += n
            if count < 128:
                value = jnp.where(lane < count, value, 0.0)
            return value

        for e in range(2):
            for k in range(NK):
                x0 = chunk(e, 2 * k)
                x1 = chunk(e, 2 * k + 1)
                f_ref[4 * w + e, 8 * k : 8 * k + 8, :] = jnp.where(upper, x0, pltpu.roll(x1, 4, 0))
                f_ref[4 * w + 2 + e, 8 * k : 8 * k + 8, :] = jnp.where(upper, pltpu.roll(x0, 4, 0), x1)
        return carry

    lax.fori_loop(0, 4, one_w, 0)


def backward_kernel(d_ref, c_ref, a_ref, o_ref, h_ref, ap_ref, y_ref):
    pad_latitude(a_ref, ap_ref)
    y_ref[...] = jnp.zeros_like(y_ref)
    lane = iota((8, 128), 1)
    upper = iota((8, 128), 0) < 4

    def one_w(w, carry):
        chunks = {}

        def chunk(e, i):
            if (e, i) not in chunks:
                k = i // 2
                t0 = d_ref[4 * w + e, 8 * k : 8 * k + 8, :]
                t1 = d_ref[4 * w + 2 + e, 8 * k : 8 * k + 8, :]
                chunks[(e, 2 * k)] = jnp.where(upper, t0, pltpu.roll(t1, 4, 0))
                chunks[(e, 2 * k + 1)] = jnp.where(upper, pltpu.roll(t0, 4, 0), t1)
            return chunks[(e, i)]

        for r in range(25):
            for j in range(4):
                first = 400 * r + 128 * j
                count = min(128, 400 - 128 * j)
                done = 0
                value = None
                while done < count:
                    e, c = divmod(first + done, 5000)
                    i, s = divmod(c, 128)
                    n = min(128 - s, 5000 - c, count - done)
                    shift = (done - s) % 128
                    piece = chunk(e, i)
                    if shift:
                        piece = pltpu.roll(piece, shift, 1)
                    value = piece if value is None else jnp.where(lane < done, value, piece)
                    done += n
                y_ref[j, pl.ds(w * 32 + r, 8, stride=YS), :] = value
        return carry

    lax.fori_loop(0, 4, one_w, 0)
    lat = split(ap_ref[...])
    lon = split(o_ref[...])
    for l in range(4):
        field = jnp.concatenate(
            [
                jnp.concatenate([y_ref[j, (4 * u + l) * YS : (4 * u + l) * YS + 128, :] for j in range(4)], axis=1)
                for u in range(2)
            ],
            axis=0,
        )
        rows = mm3(lat, split(field), TN)
        h_ref[l] = c_ref[l] + mm3(split(rows[:, :400]), lon)


def prepare_kernel(kf_ref, kl_ref, s_ref, key_ref, p_ref, v_ref, spk_ref, vb_ref, vt_ref, pp_ref):
    take = [
        (((iota((64, 128), 1) // 8) * 4 + iota((64, 128), 1) % 4 == iota((64, 128), 0)) & ((iota((64, 128), 1) // 4) % 2 == p))
        .astype(F32)
        .astype(BF16)
        for p in range(2)
    ]
    put = [(iota((128, 64), 0) == iota((128, 64), 1) + 64 * p).astype(F32).astype(BF16) for p in range(2)]
    for n, v in enumerate(split(v_ref[...])):
        big = jnp.zeros((128, 128), F32)
        for p in range(2):
            wide = mm(v, take[p], NN).astype(BF16)
            big = big + mm(put[p], wide, NN)
        vb_ref[n] = big.astype(BF16)
        vt_ref[n] = big.T.astype(BF16)

    pp_ref[:, 0:4992] = p_ref[:, 0:4992]
    pp_ref[:, 4992:5120] = jnp.zeros((256, 128), BF16)
    pp_ref[:, 4992:5000] = p_ref[:, 4992:5000]
    scale = s_ref[0]

    def one_block(b, carry):
        key = key_ref[pl.ds(b, 1), :]
        cell = key >> 8
        mine = iota((256, OB), 0) == (key & 255)
        first = jnp.minimum(kf_ref[b], NK - 2)

        def window(k, width):
            start = pl.multiple_of(k * 256, 256)
            hot = (iota((width, OB), 0) == cell - start).astype(F32).astype(BF16)
            z = mm(pp_ref[:, pl.ds(start, width)], hot, NN)
            return jnp.sum(jnp.where(mine, z, 0.0), axis=0, keepdims=True)

        total = window(first, 512)
        total = lax.fori_loop(first + 2, kl_ref[b] + 1, lambda k, t: t + window(k, 256), total)
        spk_ref[pl.ds(b, 1), :] = total * scale
        return carry

    lax.fori_loop(0, NB, one_block, 0)


def obs_parts(key, first):
    cell = (key >> 8) - first * 256
    row = ((cell >> 7) & 1) * 64 + (key & 63)
    inside = cell >= 0
    at = jnp.where(inside, (cell >> 8) * 128 + (cell & 127), -1)
    return row, at


def observe_kernel(kf_ref, kl_ref, key_ref, spk_ref, vb_ref, r_ref, out_ref, l_ref, part_ref):
    vb = (vb_ref[0], vb_ref[1])
    for k in range(NK):
        h = r_ref[:, 8 * k : 8 * k + 8, :].reshape(128, 128)
        hi, lo = split(mm3(vb, split(h)))
        l_ref[k, :, 0:128] = hi
        l_ref[k, :, 128:256] = lo

    def one_block(b, carry):
        key = key_ref[pl.ds(b, 1), :]
        first = jnp.minimum(kf_ref[b], NK - 2)
        row, at = obs_parts(key, first)
        mine = iota((128, OB), 0) == row
        hot = (iota((256, OB), 0) == at).astype(F32).astype(BF16)
        h0, h1 = hot[0:128], hot[128:256]
        z = mm(l_ref[first], jnp.concatenate([h0, h0], axis=0), NN)
        z = z + mm(l_ref[first + 1], jnp.concatenate([h1, h1], axis=0), NN)
        total = jnp.sum(jnp.where(mine, z, 0.0), axis=0, keepdims=True)

        def more(k, t):
            at_k = at - (k - first) * 128
            hk = (iota((128, OB), 0) == at_k).astype(F32).astype(BF16)
            zk = mm(l_ref[k], jnp.concatenate([hk, hk], axis=0), NN)
            return t + jnp.sum(jnp.where(mine, zk, 0.0), axis=0, keepdims=True)

        total = lax.fori_loop(first + 2, kl_ref[b] + 1, more, total)
        part_ref[pl.ds(b, 1), :] = total
        return carry

    lax.fori_loop(0, NB, one_block, 0)
    out_ref[...] = jnp.broadcast_to((part_ref[...] * spk_ref[...])[None], out_ref.shape)


def adjoint_kernel(kf_ref, kl_ref, key_ref, spk_ref, w_ref, ag_ref, vt_ref, d_ref, adj_ref, u_ref):
    adj_ref[...] = jnp.zeros_like(adj_ref)
    u_ref[...] = spk_ref[...] * (w_ref[...] * jnp.sum(ag_ref[...], axis=0))

    def one_block(b, carry):
        key = key_ref[pl.ds(b, 1), :]
        first = jnp.minimum(kf_ref[b], NK - 2)
        row, at = obs_parts(key, first)
        mine = iota((128, OB), 0) == row
        u = u_ref[pl.ds(b, 1), :]
        uh = u.astype(BF16).astype(F32)
        parts = [jnp.where(mine, x, 0.0).astype(BF16) for x in (uh, u - uh)]
        hot = (iota((256, OB), 0) == at).astype(F32).astype(BF16)
        z = mm(parts[0], hot, NT) + mm(parts[1], hot, NT)
        adj_ref[first] += z[:, 0:128]
        adj_ref[first + 1] += z[:, 128:256]

        def more(k, c):
            at_k = at - (k - first) * 128
            hk = (iota((128, OB), 0) == at_k).astype(F32).astype(BF16)
            adj_ref[k] += mm(parts[0], hk, NT) + mm(parts[1], hk, NT)
            return c

        return lax.fori_loop(first + 2, kl_ref[b] + 1, more, carry)

    lax.fori_loop(0, NB, one_block, 0)
    vt = (vt_ref[0], vt_ref[1])
    for k in range(NK):
        d_ref[:, 8 * k : 8 * k + 8, :] = mm3(vt, split(adj_ref[k])).reshape(16, 8, 128)


VM = pl.BlockSpec(memory_space=pltpu.VMEM)
SM = pl.BlockSpec(memory_space=pltpu.SMEM)


def call(kernel, outs, ins, scratch, flops, nbytes, name):
    return pl.pallas_call(
        kernel,
        out_shape=outs,
        in_specs=ins,
        out_specs=jax.tree.map(lambda _: VM, outs),
        scratch_shapes=scratch,
        compiler_params=pltpu.CompilerParams(vmem_limit_bytes=48 * 1024 * 1024),
        cost_estimate=pl.CostEstimate(flops=flops, bytes_accessed=nbytes, transcendentals=0),
        name=name,
    )


def body(
    control,
    perturbations,
    member_scales,
    vertical_loc,
    latitude_loc,
    longitude_loc,
    observed_index,
    observed_weight,
):
    sds = jax.ShapeDtypeStruct
    field_scratch = [pltpu.VMEM((256, 200), F32), pltpu.VMEM((4, 8 * YS, 128), F32)]
    c = control[0]
    flat = call(
        forward_kernel, sds((16, 160, 128), F32), [VM] * 3, field_scratch, 3_000_000_000, 4_000_000, "forward"
    )(c, latitude_loc, longitude_loc)
    columns = lax.all_to_all(flat, "lev", split_axis=0, concat_axis=0, tiled=True)

    slot = jnp.arange(2, dtype=I32)[:, None] * 128
    cell = observed_index % 5000
    key = cell * 256 + slot + observed_index // 5000
    key, weight = lax.sort((key.reshape(8192), observed_weight.reshape(8192)), num_keys=1)
    key = key.reshape(NB, OB)
    weight = weight.reshape(NB, OB)
    kf = key[:, 0] >> 16
    kl = key[:, OB - 1] >> 16
    spk, vb, vt = call(
        prepare_kernel,
        (sds((NB, OB), F32), sds((2, 128, 128), BF16), sds((2, 128, 128), BF16)),
        [SM, SM, SM, VM, VM, VM],
        [pltpu.VMEM((256, 5120), BF16)],
        4_000_000_000,
        3_000_000,
        "prepare",
    )(kf, kl, member_scales, key, perturbations.reshape(256, 5000), vertical_loc)

    copies = call(
        observe_kernel,
        sds((8, NB, OB), F32),
        [SM, SM, VM, VM, VM, VM],
        [pltpu.VMEM((NK, 128, 256), BF16), pltpu.VMEM((NB, OB), F32)],
        3_000_000_000,
        2_000_000,
        "observe",
    )(kf, kl, key, spk, vb, columns)
    gathered = lax.all_to_all(copies, "mem", split_axis=0, concat_axis=0, tiled=True)
    adjoint = call(
        adjoint_kernel,
        sds((16, 160, 128), F32),
        [SM, SM, VM, VM, VM, VM, VM],
        [pltpu.VMEM((NK, 128, 128), F32), pltpu.VMEM((NB, OB), F32)],
        3_000_000_000,
        2_000_000,
        "adjoint",
    )(kf, kl, key, spk, weight, gathered, vt)
    levels = lax.all_to_all(adjoint, "lev", split_axis=0, concat_axis=0, tiled=True)
    result = call(
        backward_kernel, sds((4, 200, 400), F32), [VM] * 4, field_scratch, 3_000_000_000, 5_000_000, "backward"
    )(levels, c, latitude_loc, longitude_loc)
    return result[None]


def solution(mesh):
    placed = (
        P("mem", "lev", None, None),
        P("mem", None, None, None, "lev"),
        P("mem"),
        P(),
        P(),
        P(),
        P(None, "lev"),
        P(None, "lev"),
    )
    return jax.shard_map(
        body, mesh=mesh, in_specs=placed, out_specs=P("mem", "lev", None, None), check_vma=False
    )
```

time: 881 us -> 100 us (0.11)
  other arithmetic: 430 us -> 7.21 us
  local copies, waits for them, and re-layouts: 186 us -> 5.3 us
  waiting for transfers between devices: 184 us -> 7.38 us
  Pallas kernels: 0 us -> 37.1 us
  matrix products: 23.6 us -> 0 us
  between operations: 14.5 us -> 0.77 us
    unnamed x5 -> x1, other arithmetic: 418 us -> 0.14 us
    psum x1 -> x0, waiting for transfers between devices: 165 us -> none  [body(): increment = lax.psum(partial_value, 'mem')]
    unnamed x23 -> x22, local copies, waits for them, and re-layouts: 125 us -> 5.27 us
    pallas_call x0 -> x5, Pallas kernels: none -> 37.1 us  [the longest x1 9.16 us: body(): call(observe_kernel, sds((8, NB, OB), F32), [SM, SM, VM, VM, VM, VM], [pl...]
    reshape x2, local copies, waits for them, and re-layouts: 31 us -> 0.02 us  [the longest x1 0.01 us: body(): key = key.reshape(NB, OB)]
    all_to_all x3 -> x0, local copies, waits for them, and re-layouts: 24.5 us -> none  [the longest x2 22.7 us: body(): lax.all_to_all(flat_fields, 'lev', split_axis=2, concat_axis=1, tiled=True)]
    dot_general x6 -> x0, matrix products: 23.6 us -> none  [the longest x1 6.47 us: body(): jnp.einsum('mlaq,oq->mlao', rows, longitude_loc, precision=HIGH)]
    all_to_all x1 -> x2, waiting for transfers between devices: 18.9 us -> 7.38 us  [the longest x1 6.16 us: body(): lax.all_to_all(copies, 'mem', split_axis=0, concat_axis=0, tiled=True)]
  transfers between devices with their start and end apart: 2 -> 2, of which waited for: 2 -> 2; matrix products, arithmetic and copies ran while one was open for 6% -> 7% of each run, Pallas kernels for 0% -> 9%
where the time goes in v1:
time: 100 us; the launch traced here: 99.6 us
  Pallas kernels  37.1 us (37%)
  blocking collectives  28.2 us (28%)
  starting transfers between devices  13.7 us (14%)
  waiting for transfers between devices  7.38 us (7%)
  other arithmetic  7.21 us (7%)
  local copies, waits for them, and re-layouts  5.3 us (5%)
    all_to_all x1, blocking collectives, body(): lax.all_to_all(adjoint, 'lev', split_axis=0, concat_axis=0, tiled=True)  28.2 us
    pallas_call x1, Pallas kernels, body(): call(observe_kernel, sds((8, NB, OB), F32), [SM, SM, VM, VM, VM, VM], [pl...  9.16 us
    pallas_call x1, Pallas kernels, body(): call(prepare_kernel, (sds((NB, OB), F32), sds((2, 128, 128), BF16), sds((...  9.14 us
    pallas_call x1, Pallas kernels, body(): call(adjoint_kernel, sds((16, 160, 128), F32), [SM, SM, VM, VM, VM, VM, V...  9.12 us
    all_to_all x1, starting transfers between devices, body(): lax.all_to_all(flat, 'lev', split_axis=0, concat_axis=0, tiled=True)  8.56 us
    sort x1, other arithmetic, body(): lax.sort((key.reshape(8192), observed_weight.reshape(8192)), num_keys=1)  6.89 us
    all_to_all x1, waiting for transfers between devices, body(): lax.all_to_all(copies, 'mem', split_axis=0, concat_axis=0, tiled=True)  6.16 us
    unnamed x22, local copies, waits for them, and re-layouts  5.27 us
  transfers between devices with their start and end apart: 2, of which 2 were waited for; matrix products, arithmetic and copies ran while one was open for 7% of the time, Pallas kernels for 9%

profile of v1, /device:TPU:1, one launch (start us, length us, event | category | flops | bytes accessed | tf_op | source)
XLA Modules:
  0.0 99.6 jit_solution(10749537053434989297)
XLA Ops:
  0.0 0.0 copy-start.1
  0.0 1.4 %copy-done.1 = f32[1,4,200,400]{3,2,1,0:T(8,128)S(1)} copy-done((f32[1,4,200,400]{3,2,1,0:T(8,128)S(1)}, f32[1,4,200,400]{3,2,1,0:T(8,128)}, u32[]{:S(2)}) %copy-start.1) | copy-done | bytes 1280024
  1.4 0.0 copy-start.3
  1.4 1.1 %copy-done.3 = f32[400,400]{1,0:T(8,128)S(1)} copy-done((f32[400,400]{1,0:T(8,128)S(1)}, f32[400,400]{1,0:T(8,128)}, u32[]{:S(2)}) %copy-start.3) | copy-done | bytes 640024
  2.6 0.0 copy-start.5
  2.6 0.9 copy-done.5
  3.5 5.0 %forward.1 = f32[16,160,128]{2,1,0:T(8,128)} custom-call(f32[4,200,400]{2,1,0:T(8,128)S(1)} %bitcast.9, f32[200,200]{1,0:T(8,128)S(1)} %copy-done.5, f32[400,400]{1,0:T(8,128)S(1)} %copy-done.3), custom_call_target="tpu_custom_call" | custom-call | flops 3000000000 | bytes 4000000 | tf_op jit(solution)/shard_map/forward/pallas_call | solution.py:297
  8.5 0.0 copy-start.8
  8.5 0.0 copy-start.9
  8.5 0.0 copy-start.7
  8.5 8.6 %all-to-all-start = ((f32[16,160,128]{2,1,0:T(8,128)}), f32[16,160,128]{2,1,0:T(8,128)S(1)}, u32[]{:S(2)}, u32[]{:S(2)}) async-start(f32[16,160,128]{2,1,0:T(8,128)} %forward.1), calls=%async_computation | async-start | bytes 2621440 | tf_op jit(solution)/shard_map/all_to_all | solution.py:300
  17.8 0.0 copy-done.8
  17.8 0.1 add_bitcast_fusion
  17.9 0.0 copy-done.9
  18.0 6.9 %sort.23 = (s32[8192]{0:T(1024)S(1)}, f32[8192]{0:T(1024)S(1)}, s32[8192]{0:T(1024)}) sort(s32[8192]{0:T(1024)S(1)} %bitcast.11, f32[8192]{0:T(1024)S(1)} %bitcast.12, s32[8192]{0:T(1024)S(1)} %iota.9), dimensions={0}, to_apply=%region_0.1 | sort | flops 106496 | bytes 196608 | tf_op jit(solution)/shard_map/sort | solution.py:305
  24.9 0.2 fusion.1
  25.0 0.0 copy-done.7
  25.1 0.0 copy-start
  25.1 1.7 %copy-done = bf16[1,2,2,64,5000]{4,3,2,1,0:T(8,128)(2,1)S(1)} copy-done((bf16[1,2,2,64,5000]{4,3,2,1,0:T(8,128)(2,1)S(1)}, bf16[1,2,2,64,5000]{4,3,2,1,0:T(8,128)(2,1)}, u32[]{:S(2)}) %copy-start) | copy-done | bytes 2560024
  26.8 9.1 %prepare.1 = (f32[32,256]{1,0:T(8,128)S(1)}, bf16[2,128,128]{2,1,0:T(8,128)(2,1)S(1)}, bf16[2,128,128]{2,1,0:T(8,128)(2,1)S(1)}) custom-call(s32[32]{0:T(128)S(1)} %get-tuple-element.18.kf_ref, s32[32]{0:T(128)S(1)} %get-tuple-element.17.kl_ref, f32[1]{0:T(128)S(6)} %copy.11.s_ref, s32[32,256]{1,0:T(8,128)S(1)} %reshape.26.key_ref, ...), custom_call_target="tpu_custom_call" | custom-call | flops 4000000000 | bytes 3000000 | tf_op jit(solution)/shard_map/prepare/pallas_call | solution.py:310
  35.9 1.2 %all-to-all-done.r_ref = f32[16,160,128]{2,1,0:T(8,128)S(1)} async-done(((f32[16,160,128]{2,1,0:T(8,128)}), f32[16,160,128]{2,1,0:T(8,128)S(1)}, u32[]{:S(2)}, u32[]{:S(2)}) %all-to-all-start) | async-done | bytes 1310752 | tf_op jit(solution)/shard_map/all_to_all | solution.py:300
  37.2 9.2 %observe.1 = f32[8,32,256]{2,1,0:T(8,128)} custom-call(s32[32]{0:T(128)S(1)} %get-tuple-element.18.kf_ref, s32[32]{0:T(128)S(1)} %get-tuple-element.17.kl_ref, s32[32,256]{1,0:T(8,128)S(1)} %reshape.26.key_ref, f32[32,256]{1,0:T(8,128)S(1)} %get-tuple-element.13.spk_ref, bf16[2,128,128]{2,1,0:T(8,128)(2,1)S(1)} %get-tuple-element.15.vb_ref, ...), custom_call_target="tpu_custom_call" | custom-call | flops 3000000000 | bytes 2000000 | tf_op jit(solution)/shard_map/observe/pallas_call | solution.py:320
  46.3 5.1 %all-to-all-start.1 = ((f32[8,32,256]{2,1,0:T(8,128)}), f32[8,32,256]{2,1,0:T(8,128)S(1)}, u32[]{:S(2)}, u32[]{:S(2)}) async-start(f32[8,32,256]{2,1,0:T(8,128)} %observe.1), calls=%async_computation.1 | async-start | bytes 524288 | tf_op jit(solution)/shard_map/all_to_all | solution.py:329
  51.5 6.2 %all-to-all-done.1.ag_ref = f32[8,32,256]{2,1,0:T(8,128)S(1)} async-done(((f32[8,32,256]{2,1,0:T(8,128)}), f32[8,32,256]{2,1,0:T(8,128)S(1)}, u32[]{:S(2)}, u32[]{:S(2)}) %all-to-all-start.1) | async-done | bytes 262176 | tf_op jit(solution)/shard_map/all_to_all | solution.py:329
  57.6 0.0 copy-start.6
  57.6 9.1 %adjoint.1 = f32[16,160,128]{2,1,0:T(8,128)S(1)} custom-call(s32[32]{0:T(128)S(1)} %get-tuple-element.18.kf_ref, s32[32]{0:T(128)S(1)} %get-tuple-element.17.kl_ref, s32[32,256]{1,0:T(8,128)S(1)} %reshape.26.key_ref, f32[32,256]{1,0:T(8,128)S(1)} %get-tuple-element.13.spk_ref, f32[32,256]{1,0:T(8,128)S(1)} %reshape.28.w_ref, ...), custom_call_target="tpu_custom_call" | custom-call | flops 3000000000 | bytes 2000000 | tf_op jit(solution)/shard_map/adjoint/pallas_call | solution.py:330
  66.8 0.0 copy-start.2
  66.8 0.0 copy-start.4
  66.8 28.2 %all_to_all.15.d_ref = f32[16,160,128]{2,1,0:T(8,128)S(1)} all-to-all(f32[16,160,128]{2,1,0:T(8,128)S(1)} %adjoint.1), channel_id=1, replica_groups=mesh['mem'=8,'lev'=16] {'lev'}, dimensions={0} | all-to-all | bytes 2621440 | tf_op jit(solution)/shard_map/all_to_all | solution.py:339
  94.9 0.0 copy-done.6
  95.0 0.0 copy-done.2
  95.0 0.0 copy-done.4
  95.0 4.6 %backward.1 = f32[4,200,400]{2,1,0:T(8,128)} custom-call(f32[16,160,128]{2,1,0:T(8,128)S(1)} %all_to_all.15.d_ref, f32[4,200,400]{2,1,0:T(8,128)S(1)} %bitcast.10, f32[200,200]{1,0:T(8,128)S(1)} %copy-done.6, f32[400,400]{1,0:T(8,128)S(1)} %copy-done.4), custom_call_target="tpu_custom_call" | custom-call | flops 3000000000 | bytes 5000000 | tf_op jit(solution)/shard_map/backward/pallas_call | solution.py:340
  (6 shorter events, 0.0 us)
Async XLA Ops:
  0.0 1.4 %copy-start.1 = (f32[1,4,200,400]{3,2,1,0:T(8,128)S(1)}, f32[1,4,200,400]{3,2,1,0:T(8,128)}, u32[]{:S(2)}) copy-start(f32[1,4,200,400]{3,2,1,0:T(8,128)} %param.8) | copy-start | bytes 3840004
  1.4 1.1 %copy-start.3 = (f32[400,400]{1,0:T(8,128)S(1)}, f32[400,400]{1,0:T(8,128)}, u32[]{:S(2)}) copy-start(f32[400,400]{1,0:T(8,128)} %o_ref.3) | copy-start | bytes 1920004
  2.6 0.9 copy-start.5
  8.5 9.2 %copy-start.8 = (s32[2,4096]{1,0:T(2,128)S(1)}, s32[2,4096]{1,0:T(2,128)}, u32[]{:S(2)}) copy-start(s32[2,4096]{1,0:T(2,128)} %param.14) | copy-start | bytes 98308
  8.5 9.4 %copy-start.9 = (f32[2,4096]{1,0:T(2,128)S(1)}, f32[2,4096]{1,0:T(2,128)}, u32[]{:S(2)}) copy-start(f32[2,4096]{1,0:T(2,128)} %param.15) | copy-start | bytes 98308
  8.5 16.5 %copy-start.7 = (f32[64,64]{1,0:T(8,128)S(1)}, f32[64,64]{1,0:T(8,128)}, u32[]{:S(2)}) copy-start(f32[64,64]{1,0:T(8,128)} %v_ref.1) | copy-start | bytes 49156
  8.5 28.6 %all-to-all-start = ((f32[16,160,128]{2,1,0:T(8,128)}), f32[16,160,128]{2,1,0:T(8,128)S(1)}, u32[]{:S(2)}, u32[]{:S(2)}) async-start(f32[16,160,128]{2,1,0:T(8,128)} %forward.1), calls=%async_computation | async-start | bytes 2621440 | tf_op jit(solution)/shard_map/all_to_all | solution.py:300
  25.1 1.7 %copy-start = (bf16[1,2,2,64,5000]{4,3,2,1,0:T(8,128)(2,1)S(1)}, bf16[1,2,2,64,5000]{4,3,2,1,0:T(8,128)(2,1)}, u32[]{:S(2)}) copy-start(bf16[1,2,2,64,5000]{4,3,2,1,0:T(8,128)(2,1)} %param.9) | copy-start | bytes 7680004
  46.3 11.3 %all-to-all-start.1 = ((f32[8,32,256]{2,1,0:T(8,128)}), f32[8,32,256]{2,1,0:T(8,128)S(1)}, u32[]{:S(2)}, u32[]{:S(2)}) async-start(f32[8,32,256]{2,1,0:T(8,128)} %observe.1), calls=%async_computation.1 | async-start | bytes 524288 | tf_op jit(solution)/shard_map/all_to_all | solution.py:329
  57.6 37.3 %copy-start.6 = (f32[200,200]{1,0:T(8,128)S(1)}, f32[200,200]{1,0:T(8,128)}, u32[]{:S(2)}) copy-start(f32[200,200]{1,0:T(8,128)} %a_ref.3) | copy-start | bytes 480004
  66.8 28.2 %copy-start.2 = (f32[1,4,200,400]{3,2,1,0:T(8,128)S(1)}, f32[1,4,200,400]{3,2,1,0:T(8,128)}, u32[]{:S(2)}) copy-start(f32[1,4,200,400]{3,2,1,0:T(8,128)} %param.8) | copy-start | bytes 3840004
  66.8 28.2 %copy-start.4 = (f32[400,400]{1,0:T(8,128)S(1)}, f32[400,400]{1,0:T(8,128)}, u32[]{:S(2)}) copy-start(f32[400,400]{1,0:T(8,128)} %o_ref.3) | copy-start | bytes 1920004

commit v2 on v1

v2 whole, which is shorter than its diff:
```python
import functools

import jax
import jax.numpy as jnp
from jax import lax
from jax.experimental import pallas as pl
from jax.experimental.pallas import tpu as pltpu
from jax.sharding import PartitionSpec as P

F32 = jnp.float32
BF16 = jnp.bfloat16
I32 = jnp.int32

NB = 32
OB = 256
NK = 20
YS = 136
NN = (((1,), (0,)), ((), ()))
NT = (((1,), (1,)), ((), ()))
TN = (((0,), (0,)), ((), ()))


def split(x):
    hi = x.astype(BF16)
    return hi, (x - hi.astype(F32)).astype(BF16)


def mm(a, b, dims):
    return lax.dot_general(a, b, dims, preferred_element_type=F32)


def mm3(a, b, dims=NN):
    return mm(a[0], b[0], dims) + (mm(a[0], b[1], dims) + mm(a[1], b[0], dims))


def pad_latitude(a_ref, ap_ref):
    ap_ref[...] = jnp.zeros_like(ap_ref)
    for i in range(8):
        row = (i % 2) * 128 + (i // 2) * 32
        ap_ref[row : row + 25, :] = a_ref[25 * i : 25 * i + 25, :]


def iota(shape, dim):
    return lax.broadcasted_iota(I32, shape, dim)


def forward_kernel(c_hbm, a_hbm, o_hbm, f_ref, lat_ref, lon_ref, ap_ref, y_ref, c_ref, a_ref, o_ref, sem):
    copies = [pltpu.make_async_copy(o_hbm, o_ref, sem.at[0])]
    copies += [pltpu.make_async_copy(c_hbm.at[l], c_ref.at[l], sem.at[2 + l]) for l in range(4)]
    copies.insert(2, pltpu.make_async_copy(a_hbm, a_ref, sem.at[1]))
    for copy in copies:
        copy.start()
    copies[0].wait()
    lon = split(o_ref[...])
    lon_ref[0], lon_ref[1] = lon
    copies[1].wait()
    rows = mm3(split(c_ref[0]), lon, NT)
    copies[2].wait()
    pad_latitude(a_ref, ap_ref)
    lat = split(ap_ref[...])
    lat_ref[0], lat_ref[1] = lat
    for l in range(4):
        if l:
            copies[2 + l].wait()
            rows = mm3(split(c_ref[l]), lon, NT)
        field = mm3(lat, split(rows))
        for u in range(2):
            base = (4 * u + l) * YS
            part = field[128 * u : 128 * u + 128]
            for j in range(3):
                y_ref[j, base : base + 128, :] = part[:, 128 * j : 128 * j + 128]
            y_ref[3, base : base + 128, 0:16] = part[:, 384:400]

    lane = iota((8, 128), 1)
    upper = iota((8, 128), 0) < 4

    def one_w(w, carry):
        loaded = {}

        def load(r, j):
            if (r, j) not in loaded:
                loaded[(r, j)] = y_ref[j, pl.ds(w * 32 + r, 8, stride=YS), :]
            return loaded[(r, j)]

        def chunk(e, i):
            first = 5000 * e + 128 * i
            count = min(128, 5000 - 128 * i)
            done = 0
            value = None
            while done < count:
                r, o = divmod(first + done, 400)
                j, s = divmod(o, 128)
                n = min(128 - s, 400 - o, count - done)
                shift = (done - s) % 128
                piece = load(r, j)
                if shift:
                    piece = pltpu.roll(piece, shift, 1)
                value = piece if value is None else jnp.where(lane < done, value, piece)
                done += n
            if count < 128:
                value = jnp.where(lane < count, value, 0.0)
            return value

        for e in range(2):
            for k in range(NK):
                x0 = chunk(e, 2 * k)
                x1 = chunk(e, 2 * k + 1)
                f_ref[4 * w + e, 8 * k : 8 * k + 8, :] = jnp.where(upper, x0, pltpu.roll(x1, 4, 0))
                f_ref[4 * w + 2 + e, 8 * k : 8 * k + 8, :] = jnp.where(upper, pltpu.roll(x0, 4, 0), x1)
        return carry

    lax.fori_loop(0, 4, one_w, 0)


def backward_kernel(d_ref, c_ref, lat_ref, lon_ref, h_ref, y_ref):
    for j in range(4):
        for g in range(8):
            for w in range(4):
                row = g * YS + w * 32 + 25
                y_ref[j, row : row + 7, :] = jnp.zeros((7, 128), F32)
    lane = iota((8, 128), 1)
    upper = iota((8, 128), 0) < 4

    def one_w(w, carry):
        chunks = {}

        def chunk(e, i):
            if (e, i) not in chunks:
                k = i // 2
                t0 = d_ref[4 * w + e, 8 * k : 8 * k + 8, :]
                t1 = d_ref[4 * w + 2 + e, 8 * k : 8 * k + 8, :]
                chunks[(e, 2 * k)] = jnp.where(upper, t0, pltpu.roll(t1, 4, 0))
                chunks[(e, 2 * k + 1)] = jnp.where(upper, pltpu.roll(t0, 4, 0), t1)
            return chunks[(e, i)]

        for r in range(25):
            for j in range(4):
                first = 400 * r + 128 * j
                count = min(128, 400 - 128 * j)
                done = 0
                value = None
                while done < count:
                    e, c = divmod(first + done, 5000)
                    i, s = divmod(c, 128)
                    n = min(128 - s, 5000 - c, count - done)
                    shift = (done - s) % 128
                    piece = chunk(e, i)
                    if shift:
                        piece = pltpu.roll(piece, shift, 1)
                    value = piece if value is None else jnp.where(lane < done, value, piece)
                    done += n
                y_ref[j, pl.ds(w * 32 + r, 8, stride=YS), :] = value
        return carry

    lax.fori_loop(0, 4, one_w, 0)
    lat = (lat_ref[0], lat_ref[1])
    lon = (lon_ref[0], lon_ref[1])
    for l in range(4):
        field = jnp.concatenate(
            [
                jnp.concatenate([y_ref[j, (4 * u + l) * YS : (4 * u + l) * YS + 128, :] for j in range(4)], axis=1)
                for u in range(2)
            ],
            axis=0,
        )
        rows = mm3(lat, split(field), TN)
        h_ref[l] = c_ref[l] + mm3(split(rows[:, :400]), lon)


def obs_parts(key, first):
    cell = (key >> 8) - first * 256
    row = ((cell >> 7) & 1) * 64 + (key & 63)
    return row, (cell >> 8) * 128 + (cell & 127)


def index_rows():
    return iota((256, OB), 0).astype(F32).astype(BF16)


def one_hot(index, at, width):
    return jnp.where(index[0:width] == at.astype(F32).astype(BF16), jnp.ones((), BF16), jnp.zeros((), BF16))


def pick(mask, z):
    return jnp.sum(jnp.where(mask, z, 0.0), axis=0, keepdims=True)


def prepare_kernel(kf_ref, kl_ref, s_ref, key_ref, p_hbm, v_ref, spk_ref, vb_ref, vt_ref, more_ref, p_ref, pp_ref, sem):
    copy = pltpu.make_async_copy(p_hbm, p_ref, sem)
    copy.start()
    take = [
        (((iota((64, 128), 1) // 8) * 4 + iota((64, 128), 1) % 4 == iota((64, 128), 0)) & ((iota((64, 128), 1) // 4) % 2 == p))
        .astype(F32)
        .astype(BF16)
        for p in range(2)
    ]
    put = [(iota((128, 64), 0) == iota((128, 64), 1) + 64 * p).astype(F32).astype(BF16) for p in range(2)]
    for n, v in enumerate(split(v_ref[...])):
        big = jnp.zeros((128, 128), F32)
        for p in range(2):
            wide = mm(v, take[p], NN).astype(BF16)
            big = big + mm(put[p], wide, NN)
        vb_ref[n] = big.astype(BF16)
        vt_ref[n] = big.T.astype(BF16)

    def one_span(b, t):
        return jnp.maximum(t, kl_ref[b] - jnp.minimum(kf_ref[b], NK - 2))

    more = lax.fori_loop(0, NB, one_span, 0, unroll=True)
    more_ref[0] = more

    copy.wait()
    for i in range(2 * NK - 1):
        pp_ref[i % 2, :, 128 * (i // 2) : 128 * (i // 2) + 128] = p_ref[:, 128 * i : 128 * i + 128]
    pp_ref[1, :, 2432:2560] = jnp.zeros((256, 128), BF16)
    pp_ref[1, :, 2432:2440] = p_ref[:, 4992:5000]
    scale = s_ref[0]
    rows = iota((256, OB), 0)
    index = index_rows()

    def select(key, start, width, hot):
        half = (key >> 15) & 1
        mine = key & 255
        lanes = pl.ds(pl.multiple_of(start * 128, 128), width)
        z = [mm(pp_ref[p, :, lanes], hot, NN) for p in range(2)]
        return pick(rows == mine, jnp.where(half == 0, z[0], z[1]))

    def one_block(b, carry):
        key = key_ref[pl.ds(b, 1), :]
        first = jnp.minimum(kf_ref[b], NK - 2)
        _, at = obs_parts(key, first)
        spk_ref[pl.ds(b, 1), :] = select(key, first, 256, one_hot(index, at, 256)) * scale
        return carry

    lax.fori_loop(0, NB, one_block, 0, unroll=4)

    @pl.when(more > 1)
    def _():
        def one_more(b, carry):
            key = key_ref[pl.ds(b, 1), :]
            first = jnp.minimum(kf_ref[b], NK - 2)

            def window(k, t):
                _, at = obs_parts(key, k)
                return t + select(key, k, 128, one_hot(index, at, 128)) * scale

            spk_ref[pl.ds(b, 1), :] = lax.fori_loop(first + 2, kl_ref[b] + 1, window, spk_ref[pl.ds(b, 1), :])
            return carry

        lax.fori_loop(0, NB, one_more, 0)


def observe_kernel(kf_ref, kl_ref, more_ref, key_ref, spk_ref, vb_ref, r_ref, out_ref, l_ref, part_ref):
    vh, vl = vb_ref[0], vb_ref[1]
    v1 = jnp.concatenate([vh, vl], axis=1)
    for k in range(0, NK, 2):
        h = [r_ref[:, 8 * (k + n) : 8 * (k + n) + 8, :].reshape(128, 128) for n in range(2)]
        hh, hl = split(jnp.concatenate(h, axis=1))
        field = mm(v1, jnp.concatenate([hh, hh], axis=0), NN) + mm(vh, hl, NN)
        hi, lo = split(field)
        l_ref[0:128, 128 * k : 128 * k + 256] = hi
        l_ref[128:256, 128 * k : 128 * k + 256] = lo
    rows = iota((128, OB), 0)
    index = index_rows()

    def value(row, start, width, hot):
        z = mm(l_ref[:, pl.ds(pl.multiple_of(start * 128, 128), width)], hot, NN)
        return pick(rows == row, z[0:128] + z[128:256])

    def one_block(b, carry):
        key = key_ref[pl.ds(b, 1), :]
        first = jnp.minimum(kf_ref[b], NK - 2)
        row, at = obs_parts(key, first)
        part_ref[pl.ds(b, 1), :] = value(row, first, 256, one_hot(index, at, 256))
        return carry

    lax.fori_loop(0, NB, one_block, 0, unroll=4)

    @pl.when(more_ref[0] > 1)
    def _():
        def one_more(b, carry):
            key = key_ref[pl.ds(b, 1), :]
            first = jnp.minimum(kf_ref[b], NK - 2)

            def window(k, t):
                row, at = obs_parts(key, k)
                return t + value(row, k, 128, one_hot(index, at, 128))

            part_ref[pl.ds(b, 1), :] = lax.fori_loop(first + 2, kl_ref[b] + 1, window, part_ref[pl.ds(b, 1), :])
            return carry

        lax.fori_loop(0, NB, one_more, 0)

    out_ref[...] = jnp.broadcast_to((part_ref[...] * spk_ref[...])[None], out_ref.shape)


def adjoint_kernel(kf_ref, kl_ref, more_ref, key_ref, spk_ref, w_ref, vt_ref, ag_ref, d_ref, adj_ref, u_ref):
    adj_ref[...] = jnp.zeros_like(adj_ref)
    u_ref[...] = spk_ref[...] * (w_ref[...] * jnp.sum(ag_ref[...], axis=0))
    index = index_rows()

    def add(row, u, start, width, hot):
        mine = index[0:128] == row.astype(F32).astype(BF16)
        parts = [jnp.where(mine, x, jnp.zeros((), BF16)) for x in split(u)]
        z = mm(jnp.concatenate(parts, axis=0), hot, NT)
        adj_ref[:, pl.ds(pl.multiple_of(start * 128, 128), width)] += z[0:128] + z[128:256]

    def one_block(b, carry):
        key = key_ref[pl.ds(b, 1), :]
        first = jnp.minimum(kf_ref[b], NK - 2)
        row, at = obs_parts(key, first)
        add(row, u_ref[pl.ds(b, 1), :], first, 256, one_hot(index, at, 256))
        return carry

    lax.fori_loop(0, NB, one_block, 0, unroll=4)

    @pl.when(more_ref[0] > 1)
    def _():
        def one_more(b, carry):
            key = key_ref[pl.ds(b, 1), :]
            first = jnp.minimum(kf_ref[b], NK - 2)

            def window(k, c):
                row, at = obs_parts(key, k)
                add(row, u_ref[pl.ds(b, 1), :], k, 128, one_hot(index, at, 128))
                return c

            return lax.fori_loop(first + 2, kl_ref[b] + 1, window, carry)

        lax.fori_loop(0, NB, one_more, 0)

    th, tl = vt_ref[0], vt_ref[1]
    t1 = jnp.concatenate([th, tl], axis=1)
    for k in range(0, NK, 2):
        ah, al = split(adj_ref[:, 128 * k : 128 * k + 256])
        d = mm(t1, jnp.concatenate([ah, ah], axis=0), NN) + mm(th, al, NN)
        for n in range(2):
            d_ref[:, 8 * (k + n) : 8 * (k + n) + 8, :] = d[:, 128 * n : 128 * n + 128].reshape(16, 8, 128)


VM = pl.BlockSpec(memory_space=pltpu.VMEM)
SM = pl.BlockSpec(memory_space=pltpu.SMEM)
HB = pl.BlockSpec(memory_space=pltpu.HBM)
DMA = pltpu.SemaphoreType.DMA


def call(kernel, outs, ins, scratch, flops, nbytes, kib, name, out_specs=None):
    return pl.pallas_call(
        kernel,
        out_shape=outs,
        in_specs=ins,
        out_specs=out_specs or jax.tree.map(lambda _: VM, outs),
        scratch_shapes=scratch,
        compiler_params=pltpu.CompilerParams(vmem_limit_bytes=kib * 1024),
        cost_estimate=pl.CostEstimate(flops=flops, bytes_accessed=nbytes, transcendentals=0),
        name=name,
    )


def body(
    control,
    perturbations,
    member_scales,
    vertical_loc,
    latitude_loc,
    longitude_loc,
    observed_index,
    observed_weight,
):
    sds = jax.ShapeDtypeStruct
    rows_scratch = pltpu.VMEM((4, 8 * YS, 128), F32)
    c = control[0]
    flat, lat, lon = call(
        forward_kernel,
        (sds((16, 160, 128), F32), sds((2, 256, 200), BF16), sds((2, 400, 400), BF16)),
        [HB] * 3,
        [
            pltpu.VMEM((256, 200), F32),
            rows_scratch,
            pltpu.VMEM((4, 200, 400), F32),
            pltpu.VMEM((200, 200), F32),
            pltpu.VMEM((400, 400), F32),
            DMA((6,)),
        ],
        3_000_000_000,
        4_000_000,
        65400,
        "forward",
    )(c, latitude_loc, longitude_loc)
    columns = lax.all_to_all(flat, "lev", split_axis=0, concat_axis=0, tiled=True)

    slot = jnp.arange(2, dtype=I32)[:, None] * 128
    cell = observed_index % 5000
    key = cell * 256 + slot + observed_index // 5000
    key, weight = lax.sort((key.reshape(8192), observed_weight.reshape(8192)), num_keys=1)
    key = key.reshape(NB, OB)
    weight = weight.reshape(NB, OB)
    kf = key[:, 0] >> 16
    kl = key[:, OB - 1] >> 16
    spk, vb, vt, more = call(
        prepare_kernel,
        (
            sds((NB, OB), F32),
            sds((2, 128, 128), BF16),
            sds((2, 128, 128), BF16),
            sds((1,), I32),
        ),
        [SM, SM, SM, VM, HB, VM],
        [pltpu.VMEM((256, 5000), BF16), pltpu.VMEM((2, 256, 2560), BF16), DMA(())],
        4_000_000_000,
        3_000_000,
        64512,
        "prepare",
        (VM, VM, VM, SM),
    )(kf, kl, member_scales, key, perturbations.reshape(256, 5000), vertical_loc)

    copies = call(
        observe_kernel,
        sds((8, NB, OB), F32),
        [SM, SM, SM, VM, VM, VM, VM],
        [pltpu.VMEM((256, NK * 128), BF16), pltpu.VMEM((NB, OB), F32)],
        3_000_000_000,
        2_000_000,
        62464,
        "observe",
    )(kf, kl, more, key, spk, vb, columns)
    gathered = lax.all_to_all(copies, "mem", split_axis=0, concat_axis=0, tiled=True)
    adjoint = call(
        adjoint_kernel,
        sds((16, 160, 128), F32),
        [SM, SM, SM, VM, VM, VM, VM, VM],
        [pltpu.VMEM((128, NK * 128), F32), pltpu.VMEM((NB, OB), F32)],
        3_000_000_000,
        2_000_000,
        24576,
        "adjoint",
    )(kf, kl, more, key, spk, weight, vt, gathered)
    levels = lax.all_to_all(adjoint, "lev", split_axis=0, concat_axis=0, tiled=True)
    result = call(
        backward_kernel, sds((4, 200, 400), F32), [VM] * 4, [rows_scratch], 3_000_000_000, 5_000_000, 24_576, "backward"
    )(levels, c, lat, lon)
    return result[None]


def solution(mesh):
    placed = (
        P("mem", "lev", None, None),
        P("mem", None, None, None, "lev"),
        P("mem"),
        P(),
        P(),
        P(),
        P(None, "lev"),
        P(None, "lev"),
    )
    return jax.shard_map(
        body, mesh=mesh, in_specs=placed, out_specs=P("mem", "lev", None, None), check_vma=False
    )
```

time: 100 us -> 89 us (0.89)
  Pallas kernels: 37.1 us -> 30.3 us
  local copies, waits for them, and re-layouts: 5.3 us -> 0.08 us
  waiting for transfers between devices: 7.38 us -> 10.4 us
  blocking collectives: 28.2 us -> 25.4 us
    unnamed x22 -> x24, local copies, waits for them, and re-layouts: 5.27 us -> 0.06 us
    pallas_call x4, Pallas kernels: 27.9 us -> 22.9 us  [the longest x1 7.65 us: body(): call(forward_kernel, (sds((16, 160, 128), F32), sds((2, 256, 200), BF16),...]
    all_to_all x1, waiting for transfers between devices: 1.21 us -> 4.2 us  [body(): lax.all_to_all(flat, 'lev', split_axis=0, concat_axis=0, tiled=True)]
    all_to_all x1, blocking collectives: 28.2 us -> 25.4 us  [body(): lax.all_to_all(adjoint, 'lev', split_axis=0, concat_axis=0, tiled=True)]
    pallas_call x1, Pallas kernels: 9.14 us -> 7.43 us  [body(): call(prepare_kernel, (sds((NB, OB), F32), sds((2, 128, 128), BF16), sds((...]
  transfers between devices with their start and end apart: 2 -> 2, of which waited for: 2 -> 2; matrix products, arithmetic and copies ran while one was open for 7% -> 9% of each run, Pallas kernels for 9% -> 8%
where the time goes in v2:
time: 89 us; the launch traced here: 88.4 us
  Pallas kernels  30.3 us (34%)
  blocking collectives  25.4 us (29%)
  starting transfers between devices  13.6 us (15%)
  waiting for transfers between devices  10.4 us (12%)
  other arithmetic  7.79 us (9%)
    all_to_all x1, blocking collectives, body(): lax.all_to_all(adjoint, 'lev', split_axis=0, concat_axis=0, tiled=True)  25.4 us
    all_to_all x1, starting transfers between devices, body(): lax.all_to_all(flat, 'lev', split_axis=0, concat_axis=0, tiled=True)  8.45 us
    pallas_call x1, Pallas kernels, body(): call(forward_kernel, (sds((16, 160, 128), F32), sds((2, 256, 200), BF16),...  7.65 us
    pallas_call x1, Pallas kernels, body(): call(prepare_kernel, (sds((NB, OB), F32), sds((2, 128, 128), BF16), sds((...  7.43 us
    sort x1, other arithmetic, body(): lax.sort((key.reshape(8192), observed_weight.reshape(8192)), num_keys=1)  6.88 us
    all_to_all x1, waiting for transfers between devices, body(): lax.all_to_all(copies, 'mem', split_axis=0, concat_axis=0, tiled=True)  6.16 us
    pallas_call x1, Pallas kernels, body(): call(observe_kernel, sds((8, NB, OB), F32), [SM, SM, SM, VM, VM, VM, VM],...  5.98 us
    all_to_all x1, starting transfers between devices, body(): lax.all_to_all(copies, 'mem', split_axis=0, concat_axis=0, tiled=True)  5.14 us
  transfers between devices with their start and end apart: 2, of which 2 were waited for; matrix products, arithmetic and copies ran while one was open for 9% of the time, Pallas kernels for 8%

profile of v2, /device:TPU:1, one launch (start us, length us, event | category | flops | bytes accessed | tf_op | source)
XLA Modules:
  0.0 88.4 jit_solution(11897346827823929749)
XLA Ops:
  0.0 7.6 %forward.1 = (f32[16,160,128]{2,1,0:T(8,128)}, bf16[2,256,200]{2,1,0:T(8,128)(2,1)}, bf16[2,400,400]{2,1,0:T(8,128)(2,1)}) custom-call(f32[4,200,400]{2,1,0:T(8,128)} %bitcast.8, f32[200,200]{1,0:T(8,128)} %a_hbm.1, f32[400,400]{1,0:T(8,128)} %o_hbm.1), custom_call_target="tpu_custom_call" | custom-call | flops 3000000000 | bytes 4000000 | tf_op jit(solution)/shard_map/forward/pallas_call | solution.py:373
  7.7 0.0 copy-start.9
  7.7 0.0 copy-start.10
  7.7 8.4 %all-to-all-start = ((f32[16,160,128]{2,1,0:T(8,128)}), f32[16,160,128]{2,1,0:T(8,128)}, u32[]{:S(2)}, u32[]{:S(2)}) async-start(f32[16,160,128]{2,1,0:T(8,128)} %get-tuple-element.22), calls=%async_computation | async-start | bytes 2621440 | tf_op jit(solution)/shard_map/all_to_all | solution.py:390
  16.8 0.0 copy-done.9
  16.8 0.1 add_bitcast_fusion
  17.0 0.0 copy-done.10
  17.0 6.9 %sort.23 = (s32[8192]{0:T(1024)S(1)}, f32[8192]{0:T(1024)S(1)}, s32[8192]{0:T(1024)}) sort(s32[8192]{0:T(1024)S(1)} %bitcast.10, f32[8192]{0:T(1024)S(1)} %bitcast.11, s32[8192]{0:T(1024)S(1)} %iota.9), dimensions={0}, to_apply=%region_0.1 | sort | flops 106496 | bytes 196608 | tf_op jit(solution)/shard_map/sort | solution.py:395
  23.9 0.0 copy-start
  23.9 0.8 fusion.1
  24.7 0.0 copy-done
  24.7 7.4 %prepare.1 = (f32[32,256]{1,0:T(8,128)}, bf16[2,128,128]{2,1,0:T(8,128)(2,1)}, bf16[2,128,128]{2,1,0:T(8,128)(2,1)}, s32[1]{0:T(128)}) custom-call(s32[32]{0:T(128)} %get-tuple-element.26.kf_ref, s32[32]{0:T(128)} %get-tuple-element.25.kl_ref, f32[1]{0:T(128)S(6)} %copy.11.s_ref, s32[32,256]{1,0:T(8,128)} %copy-done, bf16[256,5000]{1,0:T(8,128)(2,1)} %bitcast.13, ...), custom_call_target="tpu_custom_call" | custom-call | flops 4000000000 | bytes 3000000 | tf_op jit(solution)/shard_map/prepare/pallas_call | solution.py:400
  32.1 4.2 %all-to-all-done.r_ref = f32[16,160,128]{2,1,0:T(8,128)} async-done(((f32[16,160,128]{2,1,0:T(8,128)}), f32[16,160,128]{2,1,0:T(8,128)}, u32[]{:S(2)}, u32[]{:S(2)}) %all-to-all-start) | async-done | bytes 1310752 | tf_op jit(solution)/shard_map/all_to_all | solution.py:390
  36.3 0.0 copy-start.1
  36.3 0.0 copy-start.2
  36.3 0.0 copy-start.3
  36.3 0.0 copy-start.7
  36.3 0.0 copy-start.8
  36.3 6.0 %observe.1 = f32[8,32,256]{2,1,0:T(8,128)} custom-call(s32[32]{0:T(128)} %get-tuple-element.26.kf_ref, s32[32]{0:T(128)} %get-tuple-element.25.kl_ref, s32[1]{0:T(128)} %get-tuple-element.17.more_ref, s32[32,256]{1,0:T(8,128)} %copy-done, f32[32,256]{1,0:T(8,128)} %get-tuple-element.18.spk_ref, bf16[2,128,128]{2,1,0:T(8,128)(2,1)} %get-tuple-element.21.vb_ref, ...), custom_call_target="tpu_custom_call" | custom-call | flops 3000000000 | bytes 2000000 | tf_op jit(solution)/shard_map/observe/pallas_call | solution.py:417
  42.3 5.1 %all-to-all-start.1 = ((f32[8,32,256]{2,1,0:T(8,128)}), f32[8,32,256]{2,1,0:T(8,128)S(1)}, u32[]{:S(2)}, u32[]{:S(2)}) async-start(f32[8,32,256]{2,1,0:T(8,128)} %observe.1), calls=%async_computation.1 | async-start | bytes 524288 | tf_op jit(solution)/shard_map/all_to_all | solution.py:427
  47.5 6.2 %all-to-all-done.1.ag_ref = f32[8,32,256]{2,1,0:T(8,128)S(1)} async-done(((f32[8,32,256]{2,1,0:T(8,128)}), f32[8,32,256]{2,1,0:T(8,128)S(1)}, u32[]{:S(2)}, u32[]{:S(2)}) %all-to-all-start.1) | async-done | bytes 262176 | tf_op jit(solution)/shard_map/all_to_all | solution.py:427
  53.6 0.0 copy-done.1
  53.6 0.0 copy-done.2
  53.6 0.0 copy-done.3
  53.6 0.0 copy-done.7
  53.6 0.0 copy-done.8
  53.7 0.0 copy-start.6
  53.7 4.8 %adjoint.1 = f32[16,160,128]{2,1,0:T(8,128)S(1)} custom-call(s32[32]{0:T(128)S(1)} %copy-done.3, s32[32]{0:T(128)S(1)} %copy-done.2, s32[1]{0:T(128)} %get-tuple-element.17.more_ref, s32[32,256]{1,0:T(8,128)S(1)} %copy-done.1, f32[32,256]{1,0:T(8,128)S(1)} %copy-done.8, f32[32,256]{1,0:T(8,128)S(1)} %reshape.28.w_ref, bf16[2,128,128]{2,1,0:T(8,128)(2,1)S(1)} %copy-done.7, ...), custom_call_target="tpu_custom_call" | custom-call | flops 3000000000 | bytes 2000000 | tf_op jit(solution)/shard_map/adjoint/pallas_call | solution.py:428
  58.4 0.0 copy-start.4
  58.5 0.0 copy-start.5
  58.5 25.4 %all_to_all.15.d_ref = f32[16,160,128]{2,1,0:T(8,128)S(1)} all-to-all(f32[16,160,128]{2,1,0:T(8,128)S(1)} %adjoint.1), channel_id=1, replica_groups=mesh['mem'=8,'lev'=16] {'lev'}, dimensions={0} | all-to-all | bytes 2621440 | tf_op jit(solution)/shard_map/all_to_all | solution.py:438
  83.9 0.0 copy-done.6
  83.9 0.0 copy-done.4
  83.9 0.0 copy-done.5
  83.9 4.5 %backward.1 = f32[4,200,400]{2,1,0:T(8,128)} custom-call(f32[16,160,128]{2,1,0:T(8,128)S(1)} %all_to_all.15.d_ref, f32[4,200,400]{2,1,0:T(8,128)S(1)} %bitcast.9, bf16[2,256,200]{2,1,0:T(8,128)(2,1)S(1)} %copy-done.6, bf16[2,400,400]{2,1,0:T(8,128)(2,1)S(1)} %copy-done.5), custom_call_target="tpu_custom_call" | custom-call | flops 3000000000 | bytes 5000000 | tf_op jit(solution)/shard_map/backward/pallas_call | solution.py:439
  (6 shorter events, 0.0 us)
Async XLA Ops:
  7.7 9.1 %copy-start.9 = (s32[2,4096]{1,0:T(2,128)S(1)}, s32[2,4096]{1,0:T(2,128)}, u32[]{:S(2)}) copy-start(s32[2,4096]{1,0:T(2,128)} %param.14) | copy-start | bytes 98308
  7.7 9.3 %copy-start.10 = (f32[2,4096]{1,0:T(2,128)S(1)}, f32[2,4096]{1,0:T(2,128)}, u32[]{:S(2)}) copy-start(f32[2,4096]{1,0:T(2,128)} %param.15) | copy-start | bytes 98308
  7.7 28.6 %all-to-all-start = ((f32[16,160,128]{2,1,0:T(8,128)}), f32[16,160,128]{2,1,0:T(8,128)}, u32[]{:S(2)}, u32[]{:S(2)}) async-start(f32[16,160,128]{2,1,0:T(8,128)} %get-tuple-element.22), calls=%async_computation | async-start | bytes 2621440 | tf_op jit(solution)/shard_map/all_to_all | solution.py:390
  23.9 0.8 copy-start
  36.3 17.3 %copy-start.1 = (s32[32,256]{1,0:T(8,128)S(1)}, s32[32,256]{1,0:T(8,128)}, u32[]{:S(2)}) copy-start(s32[32,256]{1,0:T(8,128)} %copy-done) | copy-start | bytes 98308
  36.3 17.3 %copy-start.2 = (s32[32]{0:T(128)S(1)}, s32[32]{0:T(128)}, u32[]{:S(2)}) copy-start(s32[32]{0:T(128)} %get-tuple-element.25.kl_ref) | copy-start | bytes 388
  36.3 17.3 %copy-start.3 = (s32[32]{0:T(128)S(1)}, s32[32]{0:T(128)}, u32[]{:S(2)}) copy-start(s32[32]{0:T(128)} %get-tuple-element.26.kf_ref) | copy-start | bytes 388
  36.3 17.3 %copy-start.7 = (bf16[2,128,128]{2,1,0:T(8,128)(2,1)S(1)}, bf16[2,128,128]{2,1,0:T(8,128)(2,1)}, u32[]{:S(2)}) copy-start(bf16[2,128,128]{2,1,0:T(8,128)(2,1)} %get-tuple-element.20.vt_ref) | copy-start | bytes 196612
  36.3 17.3 %copy-start.8 = (f32[32,256]{1,0:T(8,128)S(1)}, f32[32,256]{1,0:T(8,128)}, u32[]{:S(2)}) copy-start(f32[32,256]{1,0:T(8,128)} %get-tuple-element.18.spk_ref) | copy-start | bytes 98308
  42.3 11.3 %all-to-all-start.1 = ((f32[8,32,256]{2,1,0:T(8,128)}), f32[8,32,256]{2,1,0:T(8,128)S(1)}, u32[]{:S(2)}, u32[]{:S(2)}) async-start(f32[8,32,256]{2,1,0:T(8,128)} %observe.1), calls=%async_computation.1 | async-start | bytes 524288 | tf_op jit(solution)/shard_map/all_to_all | solution.py:427
  53.7 30.3 %copy-start.6 = (bf16[2,256,200]{2,1,0:T(8,128)(2,1)S(1)}, bf16[2,256,200]{2,1,0:T(8,128)(2,1)}, u32[]{:S(2)}) copy-start(bf16[2,256,200]{2,1,0:T(8,128)(2,1)} %get-tuple-element.23.lat_ref) | copy-start | bytes 614404
  58.4 25.5 %copy-start.4 = (f32[1,4,200,400]{3,2,1,0:T(8,128)S(1)}, f32[1,4,200,400]{3,2,1,0:T(8,128)}, u32[]{:S(2)}) copy-start(f32[1,4,200,400]{3,2,1,0:T(8,128)} %param.8) | copy-start | bytes 3840004
  58.5 25.5 %copy-start.5 = (bf16[2,400,400]{2,1,0:T(8,128)(2,1)S(1)}, bf16[2,400,400]{2,1,0:T(8,128)(2,1)}, u32[]{:S(2)}) copy-start(bf16[2,400,400]{2,1,0:T(8,128)(2,1)} %get-tuple-element.24.lon_ref) | copy-start | bytes 1920004

commit v3 on v2

--- a/solution.py
+++ b/solution.py
@@ -44,35 +44,35 @@
     return lax.broadcasted_iota(I32, shape, dim)
 
 
-def forward_kernel(c_hbm, a_hbm, o_hbm, f_ref, lat_ref, lon_ref, ap_ref, y_ref, c_ref, a_ref, o_ref, sem):
-    copies = [pltpu.make_async_copy(o_hbm, o_ref, sem.at[0])]
-    copies += [pltpu.make_async_copy(c_hbm.at[l], c_ref.at[l], sem.at[2 + l]) for l in range(4)]
-    copies.insert(2, pltpu.make_async_copy(a_hbm, a_ref, sem.at[1]))
-    for copy in copies:
+def forward_kernel(c_hbm, a_hbm, o_hbm, f_hbm, f_ref, y_ref, c_ref, a_ref, o_ref, sem, out_sem):
+    reads = [
+        pltpu.make_async_copy(a_hbm, a_ref, sem.at[0]),
+        pltpu.make_async_copy(c_hbm, c_ref, sem.at[1]),
+        pltpu.make_async_copy(o_hbm, o_ref, sem.at[2]),
+    ]
+    for copy in reads:
         copy.start()
-    copies[0].wait()
+    reads[0].wait()
+    reads[1].wait()
+    lat = split(a_ref[...])
+    rows = [split(mm3(lat, split(c_ref[l]))) for l in range(4)]
+    reads[2].wait()
     lon = split(o_ref[...])
-    lon_ref[0], lon_ref[1] = lon
-    copies[1].wait()
-    rows = mm3(split(c_ref[0]), lon, NT)
-    copies[2].wait()
-    pad_latitude(a_ref, ap_ref)
-    lat = split(ap_ref[...])
-    lat_ref[0], lat_ref[1] = lat
     for l in range(4):
-        if l:
-            copies[2 + l].wait()
-            rows = mm3(split(c_ref[l]), lon, NT)
-        field = mm3(lat, split(rows))
-        for u in range(2):
-            base = (4 * u + l) * YS
-            part = field[128 * u : 128 * u + 128]
+        field = mm3(rows[l], lon, NT)
+        for i in range(8):
+            row = (4 * (i % 2) + l) * YS + 32 * (i // 2)
+            part = field[25 * i : 25 * i + 25]
             for j in range(3):
-                y_ref[j, base : base + 128, :] = part[:, 128 * j : 128 * j + 128]
-            y_ref[3, base : base + 128, 0:16] = part[:, 384:400]
+                y_ref[j, row : row + 25, :] = part[:, 128 * j : 128 * j + 128]
+            y_ref[3, row : row + 25, 0:16] = part[:, 384:400]
 
     lane = iota((8, 128), 1)
     upper = iota((8, 128), 0) < 4
+
+    def write(w):
+        blocks = pl.ds(4 * w, 4)
+        return pltpu.make_async_copy(f_ref.at[blocks], f_hbm.at[blocks], out_sem.at[w])
 
     def one_w(w, carry):
         loaded = {}
@@ -107,12 +107,15 @@
                 x1 = chunk(e, 2 * k + 1)
                 f_ref[4 * w + e, 8 * k : 8 * k + 8, :] = jnp.where(upper, x0, pltpu.roll(x1, 4, 0))
                 f_ref[4 * w + 2 + e, 8 * k : 8 * k + 8, :] = jnp.where(upper, pltpu.roll(x0, 4, 0), x1)
+        write(w).start()
         return carry
 
     lax.fori_loop(0, 4, one_w, 0)
-
-
-def backward_kernel(d_ref, c_ref, lat_ref, lon_ref, h_ref, y_ref):
+    for w in range(4):
+        write(w).wait()
+
+
+def backward_kernel(d_ref, c_ref, lat_ref, lon_ref, h_hbm, y_ref, h_ref, sem):
     for j in range(4):
         for g in range(8):
             for w in range(4):
@@ -153,6 +156,7 @@
         return carry
 
     lax.fori_loop(0, 4, one_w, 0)
+    writes = []
     lat = (lat_ref[0], lat_ref[1])
     lon = (lon_ref[0], lon_ref[1])
     for l in range(4):
@@ -165,6 +169,10 @@
         )
         rows = mm3(lat, split(field), TN)
         h_ref[l] = c_ref[l] + mm3(split(rows[:, :400]), lon)
+        writes.append(pltpu.make_async_copy(h_ref.at[l], h_hbm.at[l], sem.at[l]))
+        writes[l].start()
+    for copy in writes:
+        copy.wait()
 
 
 def obs_parts(key, first):
@@ -185,7 +193,9 @@
     return jnp.sum(jnp.where(mask, z, 0.0), axis=0, keepdims=True)
 
 
-def prepare_kernel(kf_ref, kl_ref, s_ref, key_ref, p_hbm, v_ref, spk_ref, vb_ref, vt_ref, more_ref, p_ref, pp_ref, sem):
+def prepare_kernel(
+    kf_ref, kl_ref, s_ref, key_ref, p_hbm, v_ref, spk_ref, vb_ref, vt_ref, more_ref, p_ref, pp_ref, sem
+):
     copy = pltpu.make_async_copy(p_hbm, p_ref, sem)
     copy.start()
     take = [
@@ -232,7 +242,7 @@
         spk_ref[pl.ds(b, 1), :] = select(key, first, 256, one_hot(index, at, 256)) * scale
         return carry
 
-    lax.fori_loop(0, NB, one_block, 0, unroll=4)
+    lax.fori_loop(0, NB, one_block, 0, unroll=True)
 
     @pl.when(more > 1)
     def _():
@@ -248,6 +258,13 @@
             return carry
 
         lax.fori_loop(0, NB, one_more, 0)
+
+
+def halves_kernel(after_hbm, a_ref, o_ref, lat_ref, lon_ref, done_ref, ap_ref):
+    pad_latitude(a_ref, ap_ref)
+    lat_ref[0], lat_ref[1] = split(ap_ref[...])
+    lon_ref[0], lon_ref[1] = split(o_ref[...])
+    done_ref[0] = 0
 
 
 def observe_kernel(kf_ref, kl_ref, more_ref, key_ref, spk_ref, vb_ref, r_ref, out_ref, l_ref, part_ref):
@@ -274,7 +291,7 @@
         part_ref[pl.ds(b, 1), :] = value(row, first, 256, one_hot(index, at, 256))
         return carry
 
-    lax.fori_loop(0, NB, one_block, 0, unroll=4)
+    lax.fori_loop(0, NB, one_block, 0, unroll=True)
 
     @pl.when(more_ref[0] > 1)
     def _():
@@ -294,7 +311,7 @@
     out_ref[...] = jnp.broadcast_to((part_ref[...] * spk_ref[...])[None], out_ref.shape)
 
 
-def adjoint_kernel(kf_ref, kl_ref, more_ref, key_ref, spk_ref, w_ref, vt_ref, ag_ref, d_ref, adj_ref, u_ref):
+def adjoint_kernel(kf_ref, kl_ref, more_ref, done_ref, key_ref, spk_ref, w_ref, vt_ref, ag_ref, d_ref, adj_ref, u_ref):
     adj_ref[...] = jnp.zeros_like(adj_ref)
     u_ref[...] = spk_ref[...] * (w_ref[...] * jnp.sum(ag_ref[...], axis=0))
     index = index_rows()
@@ -312,7 +329,7 @@
         add(row, u_ref[pl.ds(b, 1), :], first, 256, one_hot(index, at, 256))
         return carry
 
-    lax.fori_loop(0, NB, one_block, 0, unroll=4)
+    lax.fori_loop(0, NB, one_block, 0, unroll=True)
 
     @pl.when(more_ref[0] > 1)
     def _():
@@ -370,22 +387,24 @@
     sds = jax.ShapeDtypeStruct
     rows_scratch = pltpu.VMEM((4, 8 * YS, 128), F32)
     c = control[0]
-    flat, lat, lon = call(
+    flat = call(
         forward_kernel,
-        (sds((16, 160, 128), F32), sds((2, 256, 200), BF16), sds((2, 400, 400), BF16)),
+        sds((16, 160, 128), F32),
         [HB] * 3,
         [
-            pltpu.VMEM((256, 200), F32),
+            pltpu.VMEM((16, 160, 128), F32),
             rows_scratch,
             pltpu.VMEM((4, 200, 400), F32),
             pltpu.VMEM((200, 200), F32),
             pltpu.VMEM((400, 400), F32),
-            DMA((6,)),
+            DMA((3,)),
+            DMA((4,)),
         ],
         3_000_000_000,
         4_000_000,
-        65400,
+        64230,
         "forward",
+        HB,
     )(c, latitude_loc, longitude_loc)
     columns = lax.all_to_all(flat, "lev", split_axis=0, concat_axis=0, tiled=True)
 
@@ -406,10 +425,14 @@
             sds((1,), I32),
         ),
         [SM, SM, SM, VM, HB, VM],
-        [pltpu.VMEM((256, 5000), BF16), pltpu.VMEM((2, 256, 2560), BF16), DMA(())],
+        [
+            pltpu.VMEM((256, 5000), BF16),
+            pltpu.VMEM((2, 256, 2560), BF16),
+            DMA(()),
+        ],
         4_000_000_000,
         3_000_000,
-        64512,
+        24576,
         "prepare",
         (VM, VM, VM, SM),
     )(kf, kl, member_scales, key, perturbations.reshape(256, 5000), vertical_loc)
@@ -421,23 +444,42 @@
         [pltpu.VMEM((256, NK * 128), BF16), pltpu.VMEM((NB, OB), F32)],
         3_000_000_000,
         2_000_000,
-        62464,
+        24576,
         "observe",
     )(kf, kl, more, key, spk, vb, columns)
     gathered = lax.all_to_all(copies, "mem", split_axis=0, concat_axis=0, tiled=True)
+    lat, lon, done = call(
+        halves_kernel,
+        (sds((2, 256, 200), BF16), sds((2, 400, 400), BF16), sds((1,), I32)),
+        [HB, VM, VM],
+        [pltpu.VMEM((256, 200), F32)],
+        1_000_000,
+        2_000_000,
+        24576,
+        "halves",
+        (VM, VM, SM),
+    )(copies, latitude_loc, longitude_loc)
     adjoint = call(
         adjoint_kernel,
         sds((16, 160, 128), F32),
-        [SM, SM, SM, VM, VM, VM, VM, VM],
+        [SM, SM, SM, SM, VM, VM, VM, VM, VM],
         [pltpu.VMEM((128, NK * 128), F32), pltpu.VMEM((NB, OB), F32)],
         3_000_000_000,
         2_000_000,
         24576,
         "adjoint",
-    )(kf, kl, more, key, spk, weight, vt, gathered)
+    )(kf, kl, more, done, key, spk, weight, vt, gathered)
     levels = lax.all_to_all(adjoint, "lev", split_axis=0, concat_axis=0, tiled=True)
     result = call(
-        backward_kernel, sds((4, 200, 400), F32), [VM] * 4, [rows_scratch], 3_000_000_000, 5_000_000, 24_576, "backward"
+        backward_kernel,
+        sds((4, 200, 400), F32),
+        [VM] * 4,
+        [rows_scratch, pltpu.VMEM((4, 200, 400), F32), DMA((4,))],
+        3_000_000_000,
+        5_000_000,
+        24576,
+        "backward",
+        HB,
     )(levels, c, lat, lon)
     return result[None]
 

time: 89 us -> 83.4 us (0.937)
  Pallas kernels: 30.3 us -> 22.2 us
  local copies, waits for them, and re-layouts: 0.08 us -> 1.8 us
  waiting for transfers between devices: 10.4 us -> 11.5 us
    pallas_call x3 -> x4, Pallas kernels: 16.9 us -> 13.9 us  [the longest x1 5.52 us: body(): call(forward_kernel, sds((16, 160, 128), F32), [HB] * 3, [pltpu.VMEM((16,...]
    pallas_call x1, Pallas kernels: 7.43 us -> 4.45 us  [body(): call(prepare_kernel, (sds((NB, OB), F32), sds((2, 128, 128), BF16), sds((...]
    pallas_call x1, Pallas kernels: 5.98 us -> 3.89 us  [body(): call(observe_kernel, sds((8, NB, OB), F32), [SM, SM, SM, VM, VM, VM, VM],...]
    all_to_all x1, waiting for transfers between devices: 4.2 us -> 5.93 us  [body(): lax.all_to_all(flat, 'lev', split_axis=0, concat_axis=0, tiled=True)]
    unnamed x24 -> x16, local copies, waits for them, and re-layouts: 0.06 us -> 1.78 us
  transfers between devices with their start and end apart: 2 -> 2, of which waited for: 2 -> 2; matrix products, arithmetic and copies ran while one was open for 9% -> 9% of each run, Pallas kernels for 8% -> 6%
where the time goes in v3:
time: 83.4 us; the launch traced here: 82.9 us
  blocking collectives  25.4 us (30%)
  Pallas kernels  22.2 us (27%)
  starting transfers between devices  13.7 us (16%)
  waiting for transfers between devices  11.5 us (14%)
  other arithmetic  7.19 us (9%)
  local copies, waits for them, and re-layouts  1.8 us (2%)
  between operations  0.98 us (1%)
    all_to_all x1, blocking collectives, body(): lax.all_to_all(adjoint, 'lev', split_axis=0, concat_axis=0, tiled=True)  25.4 us
    all_to_all x1, starting transfers between devices, body(): lax.all_to_all(flat, 'lev', split_axis=0, concat_axis=0, tiled=True)  8.58 us
    sort x1, other arithmetic, body(): lax.sort((key.reshape(8192), observed_weight.reshape(8192)), num_keys=1)  6.87 us
    all_to_all x1, waiting for transfers between devices, body(): lax.all_to_all(flat, 'lev', split_axis=0, concat_axis=0, tiled=True)  5.93 us
    all_to_all x1, waiting for transfers between devices, body(): lax.all_to_all(copies, 'mem', split_axis=0, concat_axis=0, tiled=True)  5.59 us
    pallas_call x1, Pallas kernels, body(): call(forward_kernel, sds((16, 160, 128), F32), [HB] * 3, [pltpu.VMEM((16,...  5.52 us
    all_to_all x1, starting transfers between devices, body(): lax.all_to_all(copies, 'mem', split_axis=0, concat_axis=0, tiled=True)  5.15 us
    pallas_call x1, Pallas kernels, body(): call(prepare_kernel, (sds((NB, OB), F32), sds((2, 128, 128), BF16), sds((...  4.45 us
  transfers between devices with their start and end apart: 2, of which 2 were waited for; matrix products, arithmetic and copies ran while one was open for 9% of the time, Pallas kernels for 6%

profile of v3, /device:TPU:1, one launch (start us, length us, event | category | flops | bytes accessed | tf_op | source)
XLA Modules:
  0.0 82.9 jit_solution(5020889683362950053)
XLA Ops:
  0.0 5.5 %forward.1 = f32[16,160,128]{2,1,0:T(8,128)} custom-call(f32[4,200,400]{2,1,0:T(8,128)} %bitcast.9, f32[200,200]{1,0:T(8,128)} %a_ref.1, f32[400,400]{1,0:T(8,128)} %o_ref.1), custom_call_target="tpu_custom_call" | custom-call | flops 3000000000 | bytes 4000000 | tf_op jit(solution)/shard_map/forward/pallas_call | solution.py:390
  5.5 0.0 copy-start.5
  5.5 0.0 copy-start.6
  5.5 0.0 copy-start.4
  5.6 8.6 %all-to-all-start = ((f32[16,160,128]{2,1,0:T(8,128)}), f32[16,160,128]{2,1,0:T(8,128)S(1)}, u32[]{:S(2)}, u32[]{:S(2)}) async-start(f32[16,160,128]{2,1,0:T(8,128)} %forward.1), calls=%async_computation | async-start | bytes 2621440 | tf_op jit(solution)/shard_map/all_to_all | solution.py:409
  14.8 0.0 copy-done.5
  14.8 0.1 add_bitcast_fusion
  15.0 0.0 copy-done.6
  15.0 6.9 %sort.23 = (s32[8192]{0:T(1024)S(1)}, f32[8192]{0:T(1024)S(1)}, s32[8192]{0:T(1024)}) sort(s32[8192]{0:T(1024)S(1)} %bitcast.11, f32[8192]{0:T(1024)S(1)} %bitcast.12, s32[8192]{0:T(1024)S(1)} %iota.9), dimensions={0}, to_apply=%region_0.1 | sort | flops 106496 | bytes 196608 | tf_op jit(solution)/shard_map/sort | solution.py:414
  21.9 0.2 fusion.1
  22.1 0.0 copy-done.4
  22.1 0.0 copy-start.2
  22.1 1.7 %copy-done.2 = bf16[1,2,2,64,5000]{4,3,2,1,0:T(8,128)(2,1)S(1)} copy-done((bf16[1,2,2,64,5000]{4,3,2,1,0:T(8,128)(2,1)S(1)}, bf16[1,2,2,64,5000]{4,3,2,1,0:T(8,128)(2,1)}, u32[]{:S(2)}) %copy-start.2) | copy-done | bytes 2560024
  23.8 4.4 %prepare.1 = (f32[32,256]{1,0:T(8,128)S(1)}, bf16[2,128,128]{2,1,0:T(8,128)(2,1)S(1)}, bf16[2,128,128]{2,1,0:T(8,128)(2,1)S(1)}, s32[1]{0:T(128)}) custom-call(s32[32]{0:T(128)S(1)} %get-tuple-element.26.kf_ref, s32[32]{0:T(128)S(1)} %get-tuple-element.25.kl_ref, f32[1]{0:T(128)S(6)} %copy.11.s_ref, s32[32,256]{1,0:T(8,128)S(1)} %reshape.26.key_ref, ...), custom_call_target="tpu_custom_call" | custom-call | flops 4000000000 | bytes 3000000 | tf_op jit(solution)/shard_map/prepare/pallas_call | solution.py:419
  28.3 5.9 %all-to-all-done.r_ref = f32[16,160,128]{2,1,0:T(8,128)S(1)} async-done(((f32[16,160,128]{2,1,0:T(8,128)}), f32[16,160,128]{2,1,0:T(8,128)S(1)}, u32[]{:S(2)}, u32[]{:S(2)}) %all-to-all-start) | async-done | bytes 1310752 | tf_op jit(solution)/shard_map/all_to_all | solution.py:409
  34.2 0.0 copy-start
  34.2 0.0 copy-start.1
  34.2 3.9 %observe.1.after_hbm = f32[8,32,256]{2,1,0:T(8,128)} custom-call(s32[32]{0:T(128)S(1)} %get-tuple-element.26.kf_ref, s32[32]{0:T(128)S(1)} %get-tuple-element.25.kl_ref, s32[1]{0:T(128)} %get-tuple-element.17.more_ref, s32[32,256]{1,0:T(8,128)S(1)} %reshape.26.key_ref, f32[32,256]{1,0:T(8,128)S(1)} %get-tuple-element.18.spk_ref, ...), custom_call_target="tpu_custom_call" | custom-call | flops 3000000000 | bytes 2000000 | tf_op jit(solution)/shard_map/observe/pallas_call | solution.py:440
  38.1 5.1 %all-to-all-start.1 = ((f32[8,32,256]{2,1,0:T(8,128)}), f32[8,32,256]{2,1,0:T(8,128)S(1)}, u32[]{:S(2)}, u32[]{:S(2)}) async-start(f32[8,32,256]{2,1,0:T(8,128)} %observe.1.after_hbm), calls=%async_computation.1 | async-start | bytes 524288 | tf_op jit(solution)/shard_map/all_to_all | solution.py:450
  43.3 0.0 copy-done
  43.3 0.0 copy-done.1
  43.3 0.5 halves.1
  43.8 5.6 %all-to-all-done.1.ag_ref = f32[8,32,256]{2,1,0:T(8,128)S(1)} async-done(((f32[8,32,256]{2,1,0:T(8,128)}), f32[8,32,256]{2,1,0:T(8,128)S(1)}, u32[]{:S(2)}, u32[]{:S(2)}) %all-to-all-start.1) | async-done | bytes 262176 | tf_op jit(solution)/shard_map/all_to_all | solution.py:450
  49.4 3.8 %adjoint.1 = f32[16,160,128]{2,1,0:T(8,128)S(1)} custom-call(s32[32]{0:T(128)S(1)} %get-tuple-element.26.kf_ref, s32[32]{0:T(128)S(1)} %get-tuple-element.25.kl_ref, s32[1]{0:T(128)} %get-tuple-element.17.more_ref, s32[1]{0:T(128)} %get-tuple-element.20.done_ref, s32[32,256]{1,0:T(8,128)S(1)} %reshape.26.key_ref, f32[32,256]{1,0:T(8,128)S(1)} %get-tuple-element.18.spk_ref, ...), custom_call_target="tpu_custom_call" | custom-call | flops 3000000000 | bytes 2000000 | tf_op jit(solution)/shard_map/adjoint/pallas_call | solution.py:462
  53.2 0.0 copy-start.3
  53.2 25.4 %all_to_all.15.d_ref = f32[16,160,128]{2,1,0:T(8,128)S(1)} all-to-all(f32[16,160,128]{2,1,0:T(8,128)S(1)} %adjoint.1), channel_id=1, replica_groups=mesh['mem'=8,'lev'=16] {'lev'}, dimensions={0} | all-to-all | bytes 2621440 | tf_op jit(solution)/shard_map/all_to_all | solution.py:472
  78.6 0.0 copy-done.3
  78.6 4.1 %backward.1 = f32[4,200,400]{2,1,0:T(8,128)} custom-call(f32[16,160,128]{2,1,0:T(8,128)S(1)} %all_to_all.15.d_ref, f32[4,200,400]{2,1,0:T(8,128)S(1)} %bitcast.10, bf16[2,256,200]{2,1,0:T(8,128)(2,1)S(1)} %get-tuple-element.23.lat_ref, bf16[2,400,400]{2,1,0:T(8,128)(2,1)S(1)} %get-tuple-element.24.lon_ref), custom_call_target="tpu_custom_call" | custom-call | flops 3000000000 | bytes 5000000 | tf_op jit(solution)/shard_map/backward/pallas_call | solution.py:473
  (6 shorter events, 0.0 us)
Async XLA Ops:
  5.5 9.3 %copy-start.5 = (s32[2,4096]{1,0:T(2,128)S(1)}, s32[2,4096]{1,0:T(2,128)}, u32[]{:S(2)}) copy-start(s32[2,4096]{1,0:T(2,128)} %param.14) | copy-start | bytes 98308
  5.5 9.4 %copy-start.6 = (f32[2,4096]{1,0:T(2,128)S(1)}, f32[2,4096]{1,0:T(2,128)}, u32[]{:S(2)}) copy-start(f32[2,4096]{1,0:T(2,128)} %param.15) | copy-start | bytes 98308
  5.5 16.5 %copy-start.4 = (f32[64,64]{1,0:T(8,128)S(1)}, f32[64,64]{1,0:T(8,128)}, u32[]{:S(2)}) copy-start(f32[64,64]{1,0:T(8,128)} %v_ref.1) | copy-start | bytes 49156
  5.6 28.6 %all-to-all-start = ((f32[16,160,128]{2,1,0:T(8,128)}), f32[16,160,128]{2,1,0:T(8,128)S(1)}, u32[]{:S(2)}, u32[]{:S(2)}) async-start(f32[16,160,128]{2,1,0:T(8,128)} %forward.1), calls=%async_computation | async-start | bytes 2621440 | tf_op jit(solution)/shard_map/all_to_all | solution.py:409
  22.1 1.7 %copy-start.2 = (bf16[1,2,2,64,5000]{4,3,2,1,0:T(8,128)(2,1)S(1)}, bf16[1,2,2,64,5000]{4,3,2,1,0:T(8,128)(2,1)}, u32[]{:S(2)}) copy-start(bf16[1,2,2,64,5000]{4,3,2,1,0:T(8,128)(2,1)} %param.9) | copy-start | bytes 7680004
  34.2 9.1 %copy-start = (f32[400,400]{1,0:T(8,128)S(1)}, f32[400,400]{1,0:T(8,128)}, u32[]{:S(2)}) copy-start(f32[400,400]{1,0:T(8,128)} %o_ref.1) | copy-start | bytes 1920004
  34.2 9.1 %copy-start.1 = (f32[200,200]{1,0:T(8,128)S(1)}, f32[200,200]{1,0:T(8,128)}, u32[]{:S(2)}) copy-start(f32[200,200]{1,0:T(8,128)} %a_ref.1) | copy-start | bytes 480004
  38.1 11.3 %all-to-all-start.1 = ((f32[8,32,256]{2,1,0:T(8,128)}), f32[8,32,256]{2,1,0:T(8,128)S(1)}, u32[]{:S(2)}, u32[]{:S(2)}) async-start(f32[8,32,256]{2,1,0:T(8,128)} %observe.1.after_hbm), calls=%async_computation.1 | async-start | bytes 524288 | tf_op jit(solution)/shard_map/all_to_all | solution.py:450
  53.2 25.5 %copy-start.3 = (f32[1,4,200,400]{3,2,1,0:T(8,128)S(1)}, f32[1,4,200,400]{3,2,1,0:T(8,128)}, u32[]{:S(2)}) copy-start(f32[1,4,200,400]{3,2,1,0:T(8,128)} %param.8) | copy-start | bytes 3840004

commit v4 on v3

--- a/solution.py
+++ b/solution.py
@@ -44,7 +44,7 @@
     return lax.broadcasted_iota(I32, shape, dim)
 
 
-def forward_kernel(c_hbm, a_hbm, o_hbm, f_hbm, f_ref, y_ref, c_ref, a_ref, o_ref, sem, out_sem):
+def forward_kernel(c_hbm, a_hbm, o_hbm, f_hbm, f_ref, y_ref, q_ref, c_ref, a_ref, o_ref, sem, out_sem):
     reads = [
         pltpu.make_async_copy(a_hbm, a_ref, sem.at[0]),
         pltpu.make_async_copy(c_hbm, c_ref, sem.at[1]),
@@ -55,14 +55,15 @@
     reads[0].wait()
     reads[1].wait()
     lat = split(a_ref[...])
-    rows = [split(mm3(lat, split(c_ref[l]))) for l in range(4)]
+    for l in range(4):
+        q_ref[200 * l : 200 * l + 200, :] = mm3(lat, split(c_ref[l]))
     reads[2].wait()
     lon = split(o_ref[...])
+    field = mm3(split(q_ref[...]), lon, NT)
     for l in range(4):
-        field = mm3(rows[l], lon, NT)
         for i in range(8):
             row = (4 * (i % 2) + l) * YS + 32 * (i // 2)
-            part = field[25 * i : 25 * i + 25]
+            part = field[200 * l + 25 * i : 200 * l + 25 * i + 25]
             for j in range(3):
                 y_ref[j, row : row + 25, :] = part[:, 128 * j : 128 * j + 128]
             y_ref[3, row : row + 25, 0:16] = part[:, 384:400]
@@ -115,7 +116,7 @@
         write(w).wait()
 
 
-def backward_kernel(d_ref, c_ref, lat_ref, lon_ref, h_hbm, y_ref, h_ref, sem):
+def backward_kernel(d_ref, c_ref, lat_ref, lon_ref, h_hbm, y_ref, q_ref, h_ref, sem):
     for j in range(4):
         for g in range(8):
             for w in range(4):
@@ -167,8 +168,11 @@
             ],
             axis=0,
         )
-        rows = mm3(lat, split(field), TN)
-        h_ref[l] = c_ref[l] + mm3(split(rows[:, :400]), lon)
+        q_ref[200 * l : 200 * l + 200, :] = mm3(lat, split(field), TN)[:, :400]
+    for l in range(4):
+        if l % 2 == 0:
+            pair = mm3(split(q_ref[200 * l : 200 * l + 400, :]), lon)
+        h_ref[l] = c_ref[l] + pair[200 * (l % 2) : 200 * (l % 2) + 200]
         writes.append(pltpu.make_async_copy(h_ref.at[l], h_hbm.at[l], sem.at[l]))
         writes[l].start()
     for copy in writes:
@@ -194,7 +198,7 @@
 
 
 def prepare_kernel(
-    kf_ref, kl_ref, s_ref, key_ref, p_hbm, v_ref, spk_ref, vb_ref, vt_ref, more_ref, p_ref, pp_ref, sem
+    n_ref, s_ref, key_ref, p_hbm, v_ref, spk_ref, vb_ref, vt_ref, p_ref, pp_ref, sem
 ):
     copy = pltpu.make_async_copy(p_hbm, p_ref, sem)
     copy.start()
@@ -213,12 +217,6 @@
         vb_ref[n] = big.astype(BF16)
         vt_ref[n] = big.T.astype(BF16)
 
-    def one_span(b, t):
-        return jnp.maximum(t, kl_ref[b] - jnp.minimum(kf_ref[b], NK - 2))
-
-    more = lax.fori_loop(0, NB, one_span, 0, unroll=True)
-    more_ref[0] = more
-
     copy.wait()
     for i in range(2 * NK - 1):
         pp_ref[i % 2, :, 128 * (i // 2) : 128 * (i // 2) + 128] = p_ref[:, 128 * i : 128 * i + 128]
@@ -237,37 +235,36 @@
 
     def one_block(b, carry):
         key = key_ref[pl.ds(b, 1), :]
-        first = jnp.minimum(kf_ref[b], NK - 2)
+        first = jnp.minimum(n_ref[b], NK - 2)
         _, at = obs_parts(key, first)
         spk_ref[pl.ds(b, 1), :] = select(key, first, 256, one_hot(index, at, 256)) * scale
         return carry
 
     lax.fori_loop(0, NB, one_block, 0, unroll=True)
 
-    @pl.when(more > 1)
+    @pl.when(n_ref[2 * NB] > 1)
     def _():
         def one_more(b, carry):
             key = key_ref[pl.ds(b, 1), :]
-            first = jnp.minimum(kf_ref[b], NK - 2)
+            first = jnp.minimum(n_ref[b], NK - 2)
 
             def window(k, t):
                 _, at = obs_parts(key, k)
                 return t + select(key, k, 128, one_hot(index, at, 128)) * scale
 
-            spk_ref[pl.ds(b, 1), :] = lax.fori_loop(first + 2, kl_ref[b] + 1, window, spk_ref[pl.ds(b, 1), :])
+            spk_ref[pl.ds(b, 1), :] = lax.fori_loop(first + 2, n_ref[NB + b] + 1, window, spk_ref[pl.ds(b, 1), :])
             return carry
 
         lax.fori_loop(0, NB, one_more, 0)
 
 
-def halves_kernel(after_hbm, a_ref, o_ref, lat_ref, lon_ref, done_ref, ap_ref):
+def halves_kernel(after_hbm, a_ref, o_ref, lat_ref, lon_ref, ap_ref):
     pad_latitude(a_ref, ap_ref)
     lat_ref[0], lat_ref[1] = split(ap_ref[...])
     lon_ref[0], lon_ref[1] = split(o_ref[...])
-    done_ref[0] = 0
-
-
-def observe_kernel(kf_ref, kl_ref, more_ref, key_ref, spk_ref, vb_ref, r_ref, out_ref, l_ref, part_ref):
+
+
+def observe_kernel(n_ref, key_ref, spk_ref, vb_ref, r_ref, out_ref, l_ref, part_ref):
     vh, vl = vb_ref[0], vb_ref[1]
     v1 = jnp.concatenate([vh, vl], axis=1)
     for k in range(0, NK, 2):
@@ -286,24 +283,24 @@
 
     def one_block(b, carry):
         key = key_ref[pl.ds(b, 1), :]
-        first = jnp.minimum(kf_ref[b], NK - 2)
+        first = jnp.minimum(n_ref[b], NK - 2)
         row, at = obs_parts(key, first)
         part_ref[pl.ds(b, 1), :] = value(row, first, 256, one_hot(index, at, 256))
         return carry
 
     lax.fori_loop(0, NB, one_block, 0, unroll=True)
 
-    @pl.when(more_ref[0] > 1)
+    @pl.when(n_ref[2 * NB] > 1)
     def _():
         def one_more(b, carry):
             key = key_ref[pl.ds(b, 1), :]
-            first = jnp.minimum(kf_ref[b], NK - 2)
+            first = jnp.minimum(n_ref[b], NK - 2)
 
             def window(k, t):
                 row, at = obs_parts(key, k)
                 return t + value(row, k, 128, one_hot(index, at, 128))
 
-            part_ref[pl.ds(b, 1), :] = lax.fori_loop(first + 2, kl_ref[b] + 1, window, part_ref[pl.ds(b, 1), :])
+            part_ref[pl.ds(b, 1), :] = lax.fori_loop(first + 2, n_ref[NB + b] + 1, window, part_ref[pl.ds(b, 1), :])
             return carry
 
         lax.fori_loop(0, NB, one_more, 0)
@@ -311,7 +308,7 @@
     out_ref[...] = jnp.broadcast_to((part_ref[...] * spk_ref[...])[None], out_ref.shape)
 
 
-def adjoint_kernel(kf_ref, kl_ref, more_ref, done_ref, key_ref, spk_ref, w_ref, vt_ref, ag_ref, d_ref, adj_ref, u_ref):
+def adjoint_kernel(n_ref, after_hbm, key_ref, spk_ref, w_ref, vt_ref, ag_ref, d_ref, adj_ref, u_ref):
     adj_ref[...] = jnp.zeros_like(adj_ref)
     u_ref[...] = spk_ref[...] * (w_ref[...] * jnp.sum(ag_ref[...], axis=0))
     index = index_rows()
@@ -324,25 +321,25 @@
 
     def one_block(b, carry):
         key = key_ref[pl.ds(b, 1), :]
-        first = jnp.minimum(kf_ref[b], NK - 2)
+        first = jnp.minimum(n_ref[b], NK - 2)
         row, at = obs_parts(key, first)
         add(row, u_ref[pl.ds(b, 1), :], first, 256, one_hot(index, at, 256))
         return carry
 
     lax.fori_loop(0, NB, one_block, 0, unroll=True)
 
-    @pl.when(more_ref[0] > 1)
+    @pl.when(n_ref[2 * NB] > 1)
     def _():
         def one_more(b, carry):
             key = key_ref[pl.ds(b, 1), :]
-            first = jnp.minimum(kf_ref[b], NK - 2)
+            first = jnp.minimum(n_ref[b], NK - 2)
 
             def window(k, c):
                 row, at = obs_parts(key, k)
                 add(row, u_ref[pl.ds(b, 1), :], k, 128, one_hot(index, at, 128))
                 return c
 
-            return lax.fori_loop(first + 2, kl_ref[b] + 1, window, carry)
+            return lax.fori_loop(first + 2, n_ref[NB + b] + 1, window, carry)
 
         lax.fori_loop(0, NB, one_more, 0)
 
@@ -394,6 +391,7 @@
         [
             pltpu.VMEM((16, 160, 128), F32),
             rows_scratch,
+            pltpu.VMEM((800, 400), F32),
             pltpu.VMEM((4, 200, 400), F32),
             pltpu.VMEM((200, 200), F32),
             pltpu.VMEM((400, 400), F32),
@@ -416,15 +414,15 @@
     weight = weight.reshape(NB, OB)
     kf = key[:, 0] >> 16
     kl = key[:, OB - 1] >> 16
-    spk, vb, vt, more = call(
+    spans = jnp.concatenate([kf, kl, jnp.max(kl - jnp.minimum(kf, NK - 2), keepdims=True)])
+    spk, vb, vt = call(
         prepare_kernel,
         (
             sds((NB, OB), F32),
             sds((2, 128, 128), BF16),
             sds((2, 128, 128), BF16),
-            sds((1,), I32),
         ),
-        [SM, SM, SM, VM, HB, VM],
+        [SM, SM, VM, HB, VM],
         [
             pltpu.VMEM((256, 5000), BF16),
             pltpu.VMEM((2, 256, 2560), BF16),
@@ -434,47 +432,45 @@
         3_000_000,
         24576,
         "prepare",
-        (VM, VM, VM, SM),
-    )(kf, kl, member_scales, key, perturbations.reshape(256, 5000), vertical_loc)
+    )(spans, member_scales, key, perturbations.reshape(256, 5000), vertical_loc)
 
     copies = call(
         observe_kernel,
         sds((8, NB, OB), F32),
-        [SM, SM, SM, VM, VM, VM, VM],
+        [SM, VM, VM, VM, VM],
         [pltpu.VMEM((256, NK * 128), BF16), pltpu.VMEM((NB, OB), F32)],
         3_000_000_000,
         2_000_000,
         24576,
         "observe",
-    )(kf, kl, more, key, spk, vb, columns)
+    )(spans, key, spk, vb, columns)
     gathered = lax.all_to_all(copies, "mem", split_axis=0, concat_axis=0, tiled=True)
-    lat, lon, done = call(
+    lat, lon = call(
         halves_kernel,
-        (sds((2, 256, 200), BF16), sds((2, 400, 400), BF16), sds((1,), I32)),
+        (sds((2, 256, 200), BF16), sds((2, 400, 400), BF16)),
         [HB, VM, VM],
         [pltpu.VMEM((256, 200), F32)],
         1_000_000,
         2_000_000,
         24576,
         "halves",
-        (VM, VM, SM),
     )(copies, latitude_loc, longitude_loc)
     adjoint = call(
         adjoint_kernel,
         sds((16, 160, 128), F32),
-        [SM, SM, SM, SM, VM, VM, VM, VM, VM],
+        [SM, HB, VM, VM, VM, VM, VM],
         [pltpu.VMEM((128, NK * 128), F32), pltpu.VMEM((NB, OB), F32)],
         3_000_000_000,
         2_000_000,
         24576,
         "adjoint",
-    )(kf, kl, more, done, key, spk, weight, vt, gathered)
+    )(spans, lat, key, spk, weight, vt, gathered)
     levels = lax.all_to_all(adjoint, "lev", split_axis=0, concat_axis=0, tiled=True)
     result = call(
         backward_kernel,
         sds((4, 200, 400), F32),
         [VM] * 4,
-        [rows_scratch, pltpu.VMEM((4, 200, 400), F32), DMA((4,))],
+        [rows_scratch, pltpu.VMEM((800, 400), F32), pltpu.VMEM((4, 200, 400), F32), DMA((4,))],
         3_000_000_000,
         5_000_000,
         24576,

time: 83.4 us -> 80.8 us (0.969)
  Pallas kernels: 22.2 us -> 18.9 us
  other arithmetic: 7.19 us -> 8.68 us
    pallas_call x3, Pallas kernels: 8.18 us -> 5.93 us  [the longest x1 3.11 us: body(): call(observe_kernel, sds((8, NB, OB), F32), [SM, VM, VM, VM, VM], [pltpu....]
    all_to_all x1, waiting for transfers between devices: 5.93 us -> 4.97 us  [body(): lax.all_to_all(flat, 'lev', split_axis=0, concat_axis=0, tiled=True)]
  transfers between devices with their start and end apart: 2 -> 2, of which waited for: 2 -> 2; matrix products, arithmetic and copies ran while one was open for 9% -> 11% of each run, Pallas kernels for 6% -> 5%
where the time goes in v4:
time: 80.8 us; the launch traced here: 80.3 us
  blocking collectives  25.4 us (31%)
  Pallas kernels  18.9 us (23%)
  starting transfers between devices  13.7 us (17%)
  waiting for transfers between devices  10.8 us (13%)
  other arithmetic  8.68 us (11%)
  local copies, waits for them, and re-layouts  1.81 us (2%)
  between operations  0.96 us (1%)
    all_to_all x1, blocking collectives, body(): lax.all_to_all(adjoint, 'lev', split_axis=0, concat_axis=0, tiled=True)  25.4 us
    all_to_all x1, starting transfers between devices, body(): lax.all_to_all(flat, 'lev', split_axis=0, concat_axis=0, tiled=True)  8.58 us
    sort x1, other arithmetic, body(): lax.sort((key.reshape(8192), observed_weight.reshape(8192)), num_keys=1)  6.87 us
    all_to_all x1, waiting for transfers between devices, body(): lax.all_to_all(copies, 'mem', split_axis=0, concat_axis=0, tiled=True)  5.82 us
    pallas_call x1, Pallas kernels, body(): call(forward_kernel, sds((16, 160, 128), F32), [HB] * 3, [pltpu.VMEM((16,...  5.32 us
    all_to_all x1, starting transfers between devices, body(): lax.all_to_all(copies, 'mem', split_axis=0, concat_axis=0, tiled=True)  5.15 us
    all_to_all x1, waiting for transfers between devices, body(): lax.all_to_all(flat, 'lev', split_axis=0, concat_axis=0, tiled=True)  4.97 us
    pallas_call x1, Pallas kernels, body(): call(prepare_kernel, (sds((NB, OB), F32), sds((2, 128, 128), BF16), sds((...  3.93 us
  transfers between devices with their start and end apart: 2, of which 2 were waited for; matrix products, arithmetic and copies ran while one was open for 11% of the time, Pallas kernels for 5%

profile of v4, /device:TPU:1, one launch (start us, length us, event | category | flops | bytes accessed | tf_op | source)
XLA Modules:
  0.0 80.3 jit_solution(9313685944674746728)
XLA Ops:
  0.0 5.3 %forward.1 = f32[16,160,128]{2,1,0:T(8,128)} custom-call(f32[4,200,400]{2,1,0:T(8,128)} %bitcast.10, f32[200,200]{1,0:T(8,128)} %a_ref.1, f32[400,400]{1,0:T(8,128)} %o_ref.1), custom_call_target="tpu_custom_call" | custom-call | flops 3000000000 | bytes 4000000 | tf_op jit(solution)/shard_map/forward/pallas_call | solution.py:387
  5.3 0.0 copy-start.5
  5.3 0.0 copy-start.6
  5.4 0.0 copy-start.4
  5.4 8.6 %all-to-all-start = ((f32[16,160,128]{2,1,0:T(8,128)}), f32[16,160,128]{2,1,0:T(8,128)S(1)}, u32[]{:S(2)}, u32[]{:S(2)}) async-start(f32[16,160,128]{2,1,0:T(8,128)} %forward.1), calls=%async_computation | async-start | bytes 2621440 | tf_op jit(solution)/shard_map/all_to_all | solution.py:407
  14.6 0.0 copy-done.5
  14.6 0.1 add_bitcast_fusion
  14.8 0.0 copy-done.6
  14.8 6.9 %sort.23 = (s32[8192]{0:T(1024)S(1)}, f32[8192]{0:T(1024)S(1)}, s32[8192]{0:T(1024)}) sort(s32[8192]{0:T(1024)S(1)} %bitcast.12, f32[8192]{0:T(1024)S(1)} %bitcast.13, s32[8192]{0:T(1024)S(1)} %iota.9), dimensions={0}, to_apply=%region_0.1 | sort | flops 106496 | bytes 196608 | tf_op jit(solution)/shard_map/sort | solution.py:412
  21.7 0.2 fusion.2
  21.9 0.7 subtract_reduce_fusion
  22.6 0.8 pad_add_fusion.n_ref
  23.4 0.0 copy-done.4
  23.4 0.0 copy-start.2
  23.4 1.7 %copy-done.2 = bf16[1,2,2,64,5000]{4,3,2,1,0:T(8,128)(2,1)S(1)} copy-done((bf16[1,2,2,64,5000]{4,3,2,1,0:T(8,128)(2,1)S(1)}, bf16[1,2,2,64,5000]{4,3,2,1,0:T(8,128)(2,1)}, u32[]{:S(2)}) %copy-start.2) | copy-done | bytes 2560024
  25.1 3.9 %prepare.1 = (f32[32,256]{1,0:T(8,128)S(1)}, bf16[2,128,128]{2,1,0:T(8,128)(2,1)S(1)}, bf16[2,128,128]{2,1,0:T(8,128)(2,1)S(1)}) custom-call(s32[65]{0:T(128)S(1)} %pad_add_fusion.n_ref, f32[1]{0:T(128)S(6)} %copy.11.s_ref, s32[32,256]{1,0:T(8,128)S(1)} %reshape.26.key_ref, bf16[256,5000]{1,0:T(8,128)(2,1)S(1)} %bitcast.9, f32[64,64]{1,0:T(8,128)S(1)} %copy-done.4), custom_call_target="tpu_custom_call" | custom-call | flops 4000000000 | bytes 3000000 | tf_op jit(solution)/shard_map/prepare/pallas_call | solution.py:418
  29.0 5.0 %all-to-all-done.r_ref = f32[16,160,128]{2,1,0:T(8,128)S(1)} async-done(((f32[16,160,128]{2,1,0:T(8,128)}), f32[16,160,128]{2,1,0:T(8,128)S(1)}, u32[]{:S(2)}, u32[]{:S(2)}) %all-to-all-start) | async-done | bytes 1310752 | tf_op jit(solution)/shard_map/all_to_all | solution.py:407
  34.0 0.0 copy-start
  34.0 0.0 copy-start.1
  34.0 3.1 %observe.1.after_hbm = f32[8,32,256]{2,1,0:T(8,128)} custom-call(s32[65]{0:T(128)S(1)} %pad_add_fusion.n_ref, s32[32,256]{1,0:T(8,128)S(1)} %reshape.26.key_ref, f32[32,256]{1,0:T(8,128)S(1)} %get-tuple-element.15.spk_ref, bf16[2,128,128]{2,1,0:T(8,128)(2,1)S(1)} %get-tuple-element.16.vb_ref, f32[16,160,128]{2,1,0:T(8,128)S(1)} %all-to-all-done.r_ref), custom_call_target="tpu_custom_call" | custom-call | flops 3000000000 | bytes 2000000 | tf_op jit(solution)/shard_map/observe/pallas_call | solution.py:437
  37.1 5.2 %all-to-all-start.1 = ((f32[8,32,256]{2,1,0:T(8,128)}), f32[8,32,256]{2,1,0:T(8,128)S(1)}, u32[]{:S(2)}, u32[]{:S(2)}) async-start(f32[8,32,256]{2,1,0:T(8,128)} %observe.1.after_hbm), calls=%async_computation.1 | async-start | bytes 524288 | tf_op jit(solution)/shard_map/all_to_all | solution.py:447
  42.3 0.0 copy-done
  42.3 0.0 copy-done.1
  42.3 0.3 halves.1
  42.6 5.8 %all-to-all-done.1.ag_ref = f32[8,32,256]{2,1,0:T(8,128)S(1)} async-done(((f32[8,32,256]{2,1,0:T(8,128)}), f32[8,32,256]{2,1,0:T(8,128)S(1)}, u32[]{:S(2)}, u32[]{:S(2)}) %all-to-all-start.1) | async-done | bytes 262176 | tf_op jit(solution)/shard_map/all_to_all | solution.py:447
  48.5 2.5 %adjoint.1 = f32[16,160,128]{2,1,0:T(8,128)S(1)} custom-call(s32[65]{0:T(128)S(1)} %pad_add_fusion.n_ref, bf16[2,256,200]{2,1,0:T(8,128)(2,1)S(1)} %get-tuple-element.17.after_hbm.lat_ref, s32[32,256]{1,0:T(8,128)S(1)} %reshape.26.key_ref, f32[32,256]{1,0:T(8,128)S(1)} %get-tuple-element.15.spk_ref, f32[32,256]{1,0:T(8,128)S(1)} %reshape.28.w_ref, ...), custom_call_target="tpu_custom_call" | custom-call | flops 3000000000 | bytes 2000000 | tf_op jit(solution)/shard_map/adjoint/pallas_call | solution.py:458
  51.0 0.0 copy-start.3
  51.0 25.4 %all_to_all.15.d_ref = f32[16,160,128]{2,1,0:T(8,128)S(1)} all-to-all(f32[16,160,128]{2,1,0:T(8,128)S(1)} %adjoint.1), channel_id=1, replica_groups=mesh['mem'=8,'lev'=16] {'lev'}, dimensions={0} | all-to-all | bytes 2621440 | tf_op jit(solution)/shard_map/all_to_all | solution.py:468
  76.4 0.0 copy-done.3
  76.4 3.7 %backward.1 = f32[4,200,400]{2,1,0:T(8,128)} custom-call(f32[16,160,128]{2,1,0:T(8,128)S(1)} %all_to_all.15.d_ref, f32[4,200,400]{2,1,0:T(8,128)S(1)} %bitcast.11, bf16[2,256,200]{2,1,0:T(8,128)(2,1)S(1)} %get-tuple-element.17.after_hbm.lat_ref, bf16[2,400,400]{2,1,0:T(8,128)(2,1)S(1)} %get-tuple-element.20.lon_ref), custom_call_target="tpu_custom_call" | custom-call | flops 3000000000 | bytes 5000000 | tf_op jit(solution)/shard_map/backward/pallas_call | solution.py:469
  (6 shorter events, 0.0 us)
Async XLA Ops:
  5.3 9.3 %copy-start.5 = (s32[2,4096]{1,0:T(2,128)S(1)}, s32[2,4096]{1,0:T(2,128)}, u32[]{:S(2)}) copy-start(s32[2,4096]{1,0:T(2,128)} %param.14) | copy-start | bytes 98308
  5.3 9.4 %copy-start.6 = (f32[2,4096]{1,0:T(2,128)S(1)}, f32[2,4096]{1,0:T(2,128)}, u32[]{:S(2)}) copy-start(f32[2,4096]{1,0:T(2,128)} %param.15) | copy-start | bytes 98308
  5.4 18.0 %copy-start.4 = (f32[64,64]{1,0:T(8,128)S(1)}, f32[64,64]{1,0:T(8,128)}, u32[]{:S(2)}) copy-start(f32[64,64]{1,0:T(8,128)} %v_ref.1) | copy-start | bytes 49156
  5.4 28.6 %all-to-all-start = ((f32[16,160,128]{2,1,0:T(8,128)}), f32[16,160,128]{2,1,0:T(8,128)S(1)}, u32[]{:S(2)}, u32[]{:S(2)}) async-start(f32[16,160,128]{2,1,0:T(8,128)} %forward.1), calls=%async_computation | async-start | bytes 2621440 | tf_op jit(solution)/shard_map/all_to_all | solution.py:407
  23.4 1.7 %copy-start.2 = (bf16[1,2,2,64,5000]{4,3,2,1,0:T(8,128)(2,1)S(1)}, bf16[1,2,2,64,5000]{4,3,2,1,0:T(8,128)(2,1)}, u32[]{:S(2)}) copy-start(bf16[1,2,2,64,5000]{4,3,2,1,0:T(8,128)(2,1)} %param.9) | copy-start | bytes 7680004
  34.0 8.3 %copy-start = (f32[400,400]{1,0:T(8,128)S(1)}, f32[400,400]{1,0:T(8,128)}, u32[]{:S(2)}) copy-start(f32[400,400]{1,0:T(8,128)} %o_ref.1) | copy-start | bytes 1920004
  34.0 8.3 %copy-start.1 = (f32[200,200]{1,0:T(8,128)S(1)}, f32[200,200]{1,0:T(8,128)}, u32[]{:S(2)}) copy-start(f32[200,200]{1,0:T(8,128)} %a_ref.1) | copy-start | bytes 480004
  37.1 11.3 %all-to-all-start.1 = ((f32[8,32,256]{2,1,0:T(8,128)}), f32[8,32,256]{2,1,0:T(8,128)S(1)}, u32[]{:S(2)}, u32[]{:S(2)}) async-start(f32[8,32,256]{2,1,0:T(8,128)} %observe.1.after_hbm), calls=%async_computation.1 | async-start | bytes 524288 | tf_op jit(solution)/shard_map/all_to_all | solution.py:447
  51.0 25.4 %copy-start.3 = (f32[1,4,200,400]{3,2,1,0:T(8,128)S(1)}, f32[1,4,200,400]{3,2,1,0:T(8,128)}, u32[]{:S(2)}) copy-start(f32[1,4,200,400]{3,2,1,0:T(8,128)} %param.8) | copy-start | bytes 3840004

commit v5 on v4

--- a/solution.py
+++ b/solution.py
@@ -111,7 +111,7 @@
         write(w).start()
         return carry
 
-    lax.fori_loop(0, 4, one_w, 0)
+    lax.fori_loop(0, 4, one_w, 0, unroll=True)
     for w in range(4):
         write(w).wait()
 
@@ -156,7 +156,7 @@
                 y_ref[j, pl.ds(w * 32 + r, 8, stride=YS), :] = value
         return carry
 
-    lax.fori_loop(0, 4, one_w, 0)
+    lax.fori_loop(0, 4, one_w, 0, unroll=True)
     writes = []
     lat = (lat_ref[0], lat_ref[1])
     lon = (lon_ref[0], lon_ref[1])

time: 80.8 us -> 80.4 us (level)
  no operation moved by 1% of the time
where the time goes in v5:
time: 80.4 us; the launch traced here: 79.9 us
  blocking collectives  25.5 us (32%)
  Pallas kernels  18.5 us (23%)
  starting transfers between devices  13.7 us (17%)
  waiting for transfers between devices  10.8 us (13%)
  other arithmetic  8.68 us (11%)
  local copies, waits for them, and re-layouts  1.81 us (2%)
  between operations  0.96 us (1%)
    all_to_all x1, blocking collectives, body(): lax.all_to_all(adjoint, 'lev', split_axis=0, concat_axis=0, tiled=True)  25.5 us
    all_to_all x1, starting transfers between devices, body(): lax.all_to_all(flat, 'lev', split_axis=0, concat_axis=0, tiled=True)  8.58 us
    sort x1, other arithmetic, body(): lax.sort((key.reshape(8192), observed_weight.reshape(8192)), num_keys=1)  6.87 us
    all_to_all x1, waiting for transfers between devices, body(): lax.all_to_all(copies, 'mem', split_axis=0, concat_axis=0, tiled=True)  5.82 us
    pallas_call x1, Pallas kernels, body(): call(forward_kernel, sds((16, 160, 128), F32), [HB] * 3, [pltpu.VMEM((16,...  5.16 us
    all_to_all x1, starting transfers between devices, body(): lax.all_to_all(copies, 'mem', split_axis=0, concat_axis=0, tiled=True)  5.15 us
    all_to_all x1, waiting for transfers between devices, body(): lax.all_to_all(flat, 'lev', split_axis=0, concat_axis=0, tiled=True)  4.97 us
    pallas_call x1, Pallas kernels, body(): call(prepare_kernel, (sds((NB, OB), F32), sds((2, 128, 128), BF16), sds((...  3.92 us
  transfers between devices with their start and end apart: 2, of which 2 were waited for; matrix products, arithmetic and copies ran while one was open for 11% of the time, Pallas kernels for 5%

profile of v5, /device:TPU:1, one launch (start us, length us, event | category | flops | bytes accessed | tf_op | source)
XLA Modules:
  0.0 79.9 jit_solution(12348375684622400024)
XLA Ops:
  0.0 5.2 %forward.1 = f32[16,160,128]{2,1,0:T(8,128)} custom-call(f32[4,200,400]{2,1,0:T(8,128)} %bitcast.10, f32[200,200]{1,0:T(8,128)} %a_ref.1, f32[400,400]{1,0:T(8,128)} %o_ref.1), custom_call_target="tpu_custom_call" | custom-call | flops 3000000000 | bytes 4000000 | tf_op jit(solution)/shard_map/forward/pallas_call | solution.py:387
  5.2 0.0 copy-start.5
  5.2 0.0 copy-start.6
  5.2 0.0 copy-start.4
  5.2 8.6 %all-to-all-start = ((f32[16,160,128]{2,1,0:T(8,128)}), f32[16,160,128]{2,1,0:T(8,128)S(1)}, u32[]{:S(2)}, u32[]{:S(2)}) async-start(f32[16,160,128]{2,1,0:T(8,128)} %forward.1), calls=%async_computation | async-start | bytes 2621440 | tf_op jit(solution)/shard_map/all_to_all | solution.py:407
  14.4 0.0 copy-done.5
  14.4 0.1 add_bitcast_fusion
  14.6 0.0 copy-done.6
  14.6 6.9 %sort.23 = (s32[8192]{0:T(1024)S(1)}, f32[8192]{0:T(1024)S(1)}, s32[8192]{0:T(1024)}) sort(s32[8192]{0:T(1024)S(1)} %bitcast.12, f32[8192]{0:T(1024)S(1)} %bitcast.13, s32[8192]{0:T(1024)S(1)} %iota.9), dimensions={0}, to_apply=%region_0.1 | sort | flops 106496 | bytes 196608 | tf_op jit(solution)/shard_map/sort | solution.py:412
  21.5 0.2 fusion.2
  21.7 0.7 subtract_reduce_fusion
  22.4 0.8 pad_add_fusion.n_ref
  23.2 0.0 copy-done.4
  23.2 0.0 copy-start.2
  23.2 1.7 %copy-done.2 = bf16[1,2,2,64,5000]{4,3,2,1,0:T(8,128)(2,1)S(1)} copy-done((bf16[1,2,2,64,5000]{4,3,2,1,0:T(8,128)(2,1)S(1)}, bf16[1,2,2,64,5000]{4,3,2,1,0:T(8,128)(2,1)}, u32[]{:S(2)}) %copy-start.2) | copy-done | bytes 2560024
  24.9 3.9 %prepare.1 = (f32[32,256]{1,0:T(8,128)S(1)}, bf16[2,128,128]{2,1,0:T(8,128)(2,1)S(1)}, bf16[2,128,128]{2,1,0:T(8,128)(2,1)S(1)}) custom-call(s32[65]{0:T(128)S(1)} %pad_add_fusion.n_ref, f32[1]{0:T(128)S(6)} %copy.11.s_ref, s32[32,256]{1,0:T(8,128)S(1)} %reshape.26.key_ref, bf16[256,5000]{1,0:T(8,128)(2,1)S(1)} %bitcast.9, f32[64,64]{1,0:T(8,128)S(1)} %copy-done.4), custom_call_target="tpu_custom_call" | custom-call | flops 4000000000 | bytes 3000000 | tf_op jit(solution)/shard_map/prepare/pallas_call | solution.py:418
  28.9 5.0 %all-to-all-done.r_ref = f32[16,160,128]{2,1,0:T(8,128)S(1)} async-done(((f32[16,160,128]{2,1,0:T(8,128)}), f32[16,160,128]{2,1,0:T(8,128)S(1)}, u32[]{:S(2)}, u32[]{:S(2)}) %all-to-all-start) | async-done | bytes 1310752 | tf_op jit(solution)/shard_map/all_to_all | solution.py:407
  33.8 0.0 copy-start
  33.8 0.0 copy-start.1
  33.9 3.1 %observe.1.after_hbm = f32[8,32,256]{2,1,0:T(8,128)} custom-call(s32[65]{0:T(128)S(1)} %pad_add_fusion.n_ref, s32[32,256]{1,0:T(8,128)S(1)} %reshape.26.key_ref, f32[32,256]{1,0:T(8,128)S(1)} %get-tuple-element.15.spk_ref, bf16[2,128,128]{2,1,0:T(8,128)(2,1)S(1)} %get-tuple-element.16.vb_ref, f32[16,160,128]{2,1,0:T(8,128)S(1)} %all-to-all-done.r_ref), custom_call_target="tpu_custom_call" | custom-call | flops 3000000000 | bytes 2000000 | tf_op jit(solution)/shard_map/observe/pallas_call | solution.py:437
  37.0 5.1 %all-to-all-start.1 = ((f32[8,32,256]{2,1,0:T(8,128)}), f32[8,32,256]{2,1,0:T(8,128)S(1)}, u32[]{:S(2)}, u32[]{:S(2)}) async-start(f32[8,32,256]{2,1,0:T(8,128)} %observe.1.after_hbm), calls=%async_computation.1 | async-start | bytes 524288 | tf_op jit(solution)/shard_map/all_to_all | solution.py:447
  42.1 0.0 copy-done
  42.1 0.0 copy-done.1
  42.1 0.3 halves.1
  42.5 5.8 %all-to-all-done.1.ag_ref = f32[8,32,256]{2,1,0:T(8,128)S(1)} async-done(((f32[8,32,256]{2,1,0:T(8,128)}), f32[8,32,256]{2,1,0:T(8,128)S(1)}, u32[]{:S(2)}, u32[]{:S(2)}) %all-to-all-start.1) | async-done | bytes 262176 | tf_op jit(solution)/shard_map/all_to_all | solution.py:447
  48.3 2.5 %adjoint.1 = f32[16,160,128]{2,1,0:T(8,128)S(1)} custom-call(s32[65]{0:T(128)S(1)} %pad_add_fusion.n_ref, bf16[2,256,200]{2,1,0:T(8,128)(2,1)S(1)} %get-tuple-element.17.after_hbm.lat_ref, s32[32,256]{1,0:T(8,128)S(1)} %reshape.26.key_ref, f32[32,256]{1,0:T(8,128)S(1)} %get-tuple-element.15.spk_ref, f32[32,256]{1,0:T(8,128)S(1)} %reshape.28.w_ref, ...), custom_call_target="tpu_custom_call" | custom-call | flops 3000000000 | bytes 2000000 | tf_op jit(solution)/shard_map/adjoint/pallas_call | solution.py:458
  50.8 0.0 copy-start.3
  50.8 25.5 %all_to_all.15.d_ref = f32[16,160,128]{2,1,0:T(8,128)S(1)} all-to-all(f32[16,160,128]{2,1,0:T(8,128)S(1)} %adjoint.1), channel_id=1, replica_groups=mesh['mem'=8,'lev'=16] {'lev'}, dimensions={0} | all-to-all | bytes 2621440 | tf_op jit(solution)/shard_map/all_to_all | solution.py:468
  76.2 0.0 copy-done.3
  76.2 3.5 %backward.1 = f32[4,200,400]{2,1,0:T(8,128)} custom-call(f32[16,160,128]{2,1,0:T(8,128)S(1)} %all_to_all.15.d_ref, f32[4,200,400]{2,1,0:T(8,128)S(1)} %bitcast.11, bf16[2,256,200]{2,1,0:T(8,128)(2,1)S(1)} %get-tuple-element.17.after_hbm.lat_ref, bf16[2,400,400]{2,1,0:T(8,128)(2,1)S(1)} %get-tuple-element.20.lon_ref), custom_call_target="tpu_custom_call" | custom-call | flops 3000000000 | bytes 5000000 | tf_op jit(solution)/shard_map/backward/pallas_call | solution.py:469
  (6 shorter events, 0.0 us)
Async XLA Ops:
  5.2 9.3 %copy-start.5 = (s32[2,4096]{1,0:T(2,128)S(1)}, s32[2,4096]{1,0:T(2,128)}, u32[]{:S(2)}) copy-start(s32[2,4096]{1,0:T(2,128)} %param.14) | copy-start | bytes 98308
  5.2 9.4 %copy-start.6 = (f32[2,4096]{1,0:T(2,128)S(1)}, f32[2,4096]{1,0:T(2,128)}, u32[]{:S(2)}) copy-start(f32[2,4096]{1,0:T(2,128)} %param.15) | copy-start | bytes 98308
  5.2 18.0 %copy-start.4 = (f32[64,64]{1,0:T(8,128)S(1)}, f32[64,64]{1,0:T(8,128)}, u32[]{:S(2)}) copy-start(f32[64,64]{1,0:T(8,128)} %v_ref.1) | copy-start | bytes 49156
  5.2 28.6 %all-to-all-start = ((f32[16,160,128]{2,1,0:T(8,128)}), f32[16,160,128]{2,1,0:T(8,128)S(1)}, u32[]{:S(2)}, u32[]{:S(2)}) async-start(f32[16,160,128]{2,1,0:T(8,128)} %forward.1), calls=%async_computation | async-start | bytes 2621440 | tf_op jit(solution)/shard_map/all_to_all | solution.py:407
  23.2 1.7 %copy-start.2 = (bf16[1,2,2,64,5000]{4,3,2,1,0:T(8,128)(2,1)S(1)}, bf16[1,2,2,64,5000]{4,3,2,1,0:T(8,128)(2,1)}, u32[]{:S(2)}) copy-start(bf16[1,2,2,64,5000]{4,3,2,1,0:T(8,128)(2,1)} %param.9) | copy-start | bytes 7680004
  33.8 8.3 %copy-start = (f32[400,400]{1,0:T(8,128)S(1)}, f32[400,400]{1,0:T(8,128)}, u32[]{:S(2)}) copy-start(f32[400,400]{1,0:T(8,128)} %o_ref.1) | copy-start | bytes 1920004
  33.8 8.3 %copy-start.1 = (f32[200,200]{1,0:T(8,128)S(1)}, f32[200,200]{1,0:T(8,128)}, u32[]{:S(2)}) copy-start(f32[200,200]{1,0:T(8,128)} %a_ref.1) | copy-start | bytes 480004
  37.0 11.3 %all-to-all-start.1 = ((f32[8,32,256]{2,1,0:T(8,128)}), f32[8,32,256]{2,1,0:T(8,128)S(1)}, u32[]{:S(2)}, u32[]{:S(2)}) async-start(f32[8,32,256]{2,1,0:T(8,128)} %observe.1.after_hbm), calls=%async_computation.1 | async-start | bytes 524288 | tf_op jit(solution)/shard_map/all_to_all | solution.py:447
  50.8 25.5 %copy-start.3 = (f32[1,4,200,400]{3,2,1,0:T(8,128)S(1)}, f32[1,4,200,400]{3,2,1,0:T(8,128)}, u32[]{:S(2)}) copy-start(f32[1,4,200,400]{3,2,1,0:T(8,128)} %param.8) | copy-start | bytes 3840004
